TPU v7x, 768 devices: a whole 4x8x12 slice. The times are simulated.
768 devices in a mesh: seq: 32 (over y, x), mp: 24 (over z, core).
Axes of the slice: x: 4, y: 8, z: 12, core: 2. Of those that a mesh axis runs over, the one named last changes fastest.
Arguments:
- hidden: bfloat16 [4096, 4096], P('seq'), may hold values from -21 to 21
- w_query: bfloat16 [4096, 3072], P(None, 'mp'), may hold values from -0.09375 to 0.09375
- w_key: bfloat16 [4096, 768], P(None, 'mp'), may hold values from -0.09375 to 0.09375
- w_value: bfloat16 [4096, 768], P(None, 'mp'), may hold values from -0.09375 to 0.09375
- mix_before: float32 [24, 24], replicated, may hold values from -1.25 to 1.25
- mix_after: float32 [24, 24], replicated, may hold values from -1.25 to 1.25
- doc_lengths: int32 [128], replicated, may hold values from 1 to 157, as said below
- doc_owner: int32 [128], replicated, may hold values from 0 to 31, as said below
- loader_order: int32 [4096], replicated, may hold values from 0 to 4095, as said below
Outputs:
- attended: bfloat16 [5120, 3072], P('seq', 'mp')
Inputs may be any that keep to these rules, and one draw needn't show every extreme that they name: `doc_lengths`: the lengths of the documents of the packed batch in order; they sum to 4096. `doc_owner`: each shard holds 4 documents; the documents of one shard hold at most 160 tokens together, and some shard holds exactly 160. `loader_order`: A permutation of the packed positions. The 128 rows of one index of seq hold, for every shard, the floor or the ceiling of that shard's tokens divided by the size of seq; so at most 5 rows for one shard, a bound that is reached.
All inputs are finite; a program needn't handle non-finite values.
Results may differ from a plain program's by a relative error of at most 0.012.
The roundings to bfloat16 on the way count: a program that leaves them out, or rounds other values in their place, can miss the bound.
Values may be sent and summed in bfloat16 or wider, within the bound.
No kernel may reach another device: no remote copies, remote signals or barrier semaphores. Data moves between devices by JAX's collectives and lax.ppermute only.
A program may use at most 32 MiB of HBM per device.

v0:
```python
import jax
import jax.numpy as jnp
from jax import lax
from jax.sharding import PartitionSpec as P

THETA = 500000.0


def rotate(values, positions, first_col, head_dim):
    columns = first_col + jnp.arange(values.shape[1])
    within = columns % head_dim
    pair_index = (within // 2).astype(jnp.float32)
    inv_freq = THETA ** (-2.0 * pair_index / head_dim)
    angle = positions[:, None].astype(jnp.float32) * inv_freq[None, :]
    partner = values.reshape(values.shape[0], values.shape[1] // 2, 2)[:, :, ::-1]
    partner = (partner * jnp.array([-1.0, 1.0], jnp.float32)).reshape(values.shape)
    return values * jnp.cos(angle) + partner * jnp.sin(angle)


def on_device(
    hidden, w_query, w_key, w_value, mix_before, mix_after, doc_lengths, doc_owner, loader_order
):
    seq_count = lax.axis_size("seq")
    seq_rank = lax.axis_index("seq")
    my_head = lax.axis_index("mp")
    tok_rows = hidden.shape[0]
    head_count = mix_before.shape[0]
    head_dim = w_query.shape[1]
    kv_cols = w_key.shape[1]
    kv_heads = head_count * kv_cols // head_dim
    group_size = head_count // kv_heads
    all_rows = loader_order.shape[0]
    doc_count = doc_lengths.shape[0]
    capacity = tok_rows * 5 // 4
    send_cap = (capacity + seq_count - 1) // seq_count
    highest = lax.Precision.HIGHEST
    doc_ends = jnp.cumsum(doc_lengths)
    starts = doc_ends - doc_lengths
    doc_index = jnp.arange(doc_count, dtype=jnp.int32)
    same_shard = doc_owner[:, None] == doc_owner[None, :]
    before = doc_index[None, :] < doc_index[:, None]
    shard_start = jnp.sum(jnp.where(same_shard & before, doc_lengths[None, :], 0), axis=1)
    inside = (loader_order[:, None] >= starts[None, :]) & (
        loader_order[:, None] < doc_ends[None, :]
    )
    target = jnp.sum(jnp.where(inside, doc_owner[None, :], 0), axis=1)
    doc_pos = loader_order - jnp.sum(jnp.where(inside, starts[None, :], 0), axis=1)
    slot_pos = jnp.sum(jnp.where(inside, shard_start[None, :], 0), axis=1) + doc_pos
    onehot = (target[:, None] == jnp.arange(seq_count, dtype=jnp.int32)[None, :]).astype(jnp.int32)
    blocked = onehot.reshape(seq_count, tok_rows, seq_count)
    counts = jnp.cumsum(blocked, axis=1) - blocked
    row_rank = jnp.sum(counts * blocked, axis=2).reshape(all_rows)
    source = jnp.arange(all_rows, dtype=jnp.int32) // tok_rows
    my_target = lax.dynamic_slice_in_dim(target, seq_rank * tok_rows, tok_rows)
    my_rank = lax.dynamic_slice_in_dim(row_rank, seq_rank * tok_rows, tok_rows)
    my_pos = lax.dynamic_slice_in_dim(doc_pos, seq_rank * tok_rows, tok_rows)
    query_rows = rotate(
        jnp.dot(hidden, w_query, preferred_element_type=jnp.float32), my_pos, 0, head_dim
    ).astype(jnp.bfloat16)
    key_rows = rotate(
        jnp.dot(hidden, w_key, preferred_element_type=jnp.float32),
        my_pos,
        my_head * kv_cols,
        head_dim,
    ).astype(jnp.bfloat16)
    value_rows = jnp.dot(hidden, w_value, preferred_element_type=jnp.float32).astype(jnp.bfloat16)
    send_at = my_target * send_cap + my_rank
    outgoing_q = (
        jnp.zeros((seq_count * send_cap, head_dim), jnp.bfloat16).at[send_at].set(query_rows)
    )
    outgoing_k = jnp.zeros((seq_count * send_cap, kv_cols), jnp.bfloat16).at[send_at].set(key_rows)
    outgoing_v = (
        jnp.zeros((seq_count * send_cap, kv_cols), jnp.bfloat16).at[send_at].set(value_rows)
    )
    got_q, got_k, got_v = (
        lax.all_to_all(outgoing_q, "seq", split_axis=0, concat_axis=0, tiled=True),
        lax.all_to_all(outgoing_k, "seq", split_axis=0, concat_axis=0, tiled=True),
        lax.all_to_all(outgoing_v, "seq", split_axis=0, concat_axis=0, tiled=True),
    )
    recv_at = jnp.where(target == seq_rank, source * send_cap + row_rank, seq_count * send_cap)
    slot_of = (
        jnp.full((seq_count * send_cap,), capacity, jnp.int32)
        .at[recv_at]
        .set(slot_pos, mode="drop")
    )
    query_slots = jnp.zeros((capacity, head_dim), jnp.bfloat16).at[slot_of].set(got_q, mode="drop")
    key_slots = jnp.zeros((capacity, kv_cols), jnp.bfloat16).at[slot_of].set(got_k, mode="drop")
    value_slots = jnp.zeros((capacity, kv_cols), jnp.bfloat16).at[slot_of].set(got_v, mode="drop")
    tslots = jnp.arange(capacity, dtype=jnp.int32)
    own_docs = doc_owner == seq_rank
    slot_held = (
        own_docs[None, :]
        & (tslots[:, None] >= shard_start[None, :])
        & (tslots[:, None] < shard_start[None, :] + doc_lengths[None, :])
    )
    filled = jnp.any(slot_held, axis=1)
    slot_doc = jnp.where(filled, jnp.sum(jnp.where(slot_held, doc_index[None, :], 0), axis=1), -1)
    attend_mask = (
        (slot_doc[:, None] == slot_doc[None, :])
        & filled[:, None]
        & (tslots[None, :] <= tslots[:, None])
    )
    score_scale = 1.0 / head_dim**0.5
    all_k, all_v = (
        lax.all_gather(key_slots, "mp", axis=1, tiled=True),
        lax.all_gather(value_slots, "mp", axis=1, tiled=True),
    )
    own_k = lax.dynamic_slice_in_dim(all_k, my_head // group_size * head_dim, head_dim, 1)
    own_logits = (
        jnp.einsum("td,ud->tu", query_slots, own_k, preferred_element_type=jnp.float32)
        * score_scale
    )
    mix_row = lax.dynamic_slice_in_dim(mix_before, my_head, 1, 0)[0]
    coeffs = mix_row
    mixed = lax.psum_scatter(
        (coeffs[:, None, None] * own_logits[None]).reshape(
            capacity * lax.axis_size("mp"), capacity
        ),
        "mp",
        scatter_dimension=0,
        tiled=True,
    )
    masked = jnp.where(attend_mask, mixed, -1e30)
    row_max = jnp.max(masked, axis=1, keepdims=True)
    expo_vals = jnp.where(attend_mask, jnp.exp(masked - row_max), 0.0)
    row_sum = jnp.sum(expo_vals, axis=1, keepdims=True)
    row_sum = jnp.where(filled[:, None], row_sum, 1.0)
    weights = (expo_vals / row_sum).astype(jnp.bfloat16)
    spread = jnp.dot(weights, all_v, preferred_element_type=jnp.float32).reshape(
        capacity, kv_heads, head_dim
    )
    after_row = lax.dynamic_slice_in_dim(mix_after, my_head, 1, 0)[0]
    head_span = capacity * lax.axis_size("mp") // capacity
    targets = jnp.arange(head_span)
    coeffs = after_row
    chooser = (targets[:, None] // group_size == jnp.arange(kv_heads)[None, :]).astype(
        jnp.float32
    ) * coeffs[:, None]
    result = lax.psum_scatter(
        jnp.einsum("kg,tgd->ktd", chooser, spread, precision=highest).reshape(
            capacity * lax.axis_size("mp"), head_dim
        ),
        "mp",
        scatter_dimension=0,
        tiled=True,
    )
    return result.astype(jnp.bfloat16)


def solution(mesh):
    placed = (P("seq", None), P(None, "mp"), P(None, "mp"), P(None, "mp"), P(), P(), P(), P(), P())
    return jax.shard_map(
        on_device, mesh=mesh, in_specs=placed, out_specs=P("seq", "mp"), check_vma=False
    )
```

profile of v0, /device:TPU:1, one launch (start us, length us, event | category | flops | bytes accessed | tf_op | source)
XLA Modules:
  0.0 293.6 jit_solution(10183812555941452400)
XLA Ops:
  6.5 1.0 select_reduce_fusion.4
  7.6 0.8 copy.51
  8.3 0.2 reduce-window.8
  8.6 0.7 fusion.56
  9.3 3.1 %select_reduce_fusion = (s32[4096]{0:T(1024)S(1)}, s32[4096]{0:T(1024)S(1)}, s32[4096]{0:T(1024)S(1)}) fusion(s32[128]{0:T(128)S(1)} %reduce, s32[128]{0:T(128)S(1)} %get-tuple-element.11, s32[4096]{0:T(1024)} %param.19, s32[128]{0:T(128)S(1)} %select_reduce_fusion.4, s32[128]{0:T(128)} %param.18), kind=kLoop, calls=%fused_computation.12 | loop fusion | flops 4706304 | bytes 67584 | tf_op jit(solution)/shard_map/reduce_sum | solution.py:47
  12.5 3.3 %fusion.3 = s32[32,128]{0,1:T(8,128)S(1)} fusion(s32[32,128]{0,1:T(8,128)S(1)} %copy.52), kind=kOutput, calls=%fused_computation.11 | output fusion | flops 17559552 | bytes 32768 | tf_op jit(solution)/shard_map/jit(cumsum)/reduce_window_sum | solution.py:51
  15.9 1.4 fusion.58
  17.6 0.1 fusion.36
  17.7 0.1 copy.56
  17.9 0.9 scatter_custom_fusion.3
  18.7 0.6 all_to_all.27
  19.4 10.5 %all-to-all-start.1 = ((bf16[32,5,32]{2,1,0:T(8,128)(2,1)}), bf16[32,5,32]{2,1,0:T(8,128)(2,1)S(1)}, u32[]{:S(2)}, u32[]{:S(2)}) async-start(bf16[32,5,32]{2,1,0:T(8,128)(2,1)} %all_to_all.27), calls=%async_computation.1 | async-start | bytes 131072 | tf_op jit(solution)/shard_map/all_to_all | solution.py:77
  30.0 15.5 %scatter_custom_fusion = s32[160]{0:T(256)S(1)} fusion(s32[4096]{0:T(1024)S(1)} %bitcast.37, s32[4096]{0:T(1024)S(1)} %get-tuple-element.8, s32[]{:T(128)} %constant.133.clone.1), kind=kCustom, calls=%fused_computation.112 | custom fusion | bytes 644 | tf_op jit(solution)/shard_map/scatter | solution.py:84
  45.5 0.5 fusion.57
  46.0 0.2 rev.6
  46.3 0.3 fusion.17
  46.6 0.7 fusion.48
  47.4 0.9 scatter_custom_fusion.1
  48.3 0.6 all_to_all.24
  49.1 9.2 %all-to-all-start = ((bf16[32,5,128]{2,1,0:T(8,128)(2,1)}), bf16[32,5,128]{2,1,0:T(8,128)(2,1)S(1)}, u32[]{:S(2)}, u32[]{:S(2)}) async-start(bf16[32,5,128]{2,1,0:T(8,128)(2,1)} %all_to_all.24), calls=%async_computation | async-start | bytes 131072 | tf_op jit(solution)/shard_map/all_to_all | solution.py:76
  58.4 0.9 scatter_custom_fusion.4
  59.4 35.5 %all_gather.6 = bf16[160,768]{0,1:T(8,128)(2,1)S(1)} all-gather(bf16[160,32]{0,1:T(8,128)(2,1)S(1)} %copy.57), channel_id=1, replica_groups=mesh['seq'=32,'mp'=24] {'mp'}, dimensions={1}, use_global_device_ids=true | all-gather | bytes 256000 | tf_op jit(solution)/shard_map/all_gather | solution.py:105
  95.0 1.1 scatter_custom_fusion.2
  96.1 0.2 convolution_multiply_fusion
  96.4 2.1 mul.162
  98.5 3.8 %mul.163 = f32[3840,160]{0,1:T(8,128)S(1)} reshape(f32[24,160,160]{1,0,2:T(8,128)} %mul.162) | data formatting | bytes 4915200 | tf_op jit(solution)/shard_map/mul | solution.py:116
  102.4 1.6 broadcast_multiply_fusion
  103.9 4.8 %copy.64 = f32[3840,160]{1,0:T(8,128)} copy(f32[3840,160]{0,1:T(8,128)} %broadcast_multiply_fusion) | data formatting | bytes 4915200
  108.8 0.9 copy-done.2
  109.7 0.4 convolution_convert_fusion
  110.1 0.1 copy.61
  110.3 0.9 scatter_custom_fusion.5
  111.1 0.6 all_to_all.30
  111.8 9.5 %all-to-all-start.2 = ((bf16[32,5,32]{2,1,0:T(8,128)(2,1)}), bf16[32,5,32]{2,1,0:T(8,128)(2,1)S(1)}, u32[]{:S(2)}, u32[]{:S(2)}) async-start(bf16[32,5,32]{2,1,0:T(8,128)(2,1)} %all_to_all.30), calls=%async_computation.2 | async-start | bytes 131072 | tf_op jit(solution)/shard_map/all_to_all | solution.py:78
  121.5 0.1 select_reduce_fusion.3
  121.6 0.7 fusion.47
  122.3 7.8 %all-to-all-done.2 = bf16[32,5,32]{2,1,0:T(8,128)(2,1)S(1)} async-done(((bf16[32,5,32]{2,1,0:T(8,128)(2,1)}), bf16[32,5,32]{2,1,0:T(8,128)(2,1)S(1)}, u32[]{:S(2)}, u32[]{:S(2)}) %all-to-all-start.2) | async-done | bytes 10272 | tf_op jit(solution)/shard_map/all_to_all | solution.py:78
  130.2 0.9 scatter_custom_fusion.6
  131.2 23.2 %all_gather.7 = bf16[160,768]{0,1:T(8,128)(2,1)S(1)} all-gather(bf16[160,32]{0,1:T(8,128)(2,1)S(1)} %copy.62), channel_id=1, replica_groups=mesh['seq'=32,'mp'=24] {'mp'}, dimensions={1}, use_global_device_ids=true | all-gather | bytes 256000 | tf_op jit(solution)/shard_map/all_gather | solution.py:106
  154.4 39.4 %reduce-scatter.7.cloned.1.call-done = f32[160,160]{1,0:T(8,128)} async-done(((f32[3840,160]{1,0:T(8,128)}), f32[160,160]{1,0:T(8,128)}) %reduce-scatter.7.cloned.1.call-update) | async-done | bytes 102416
  193.8 1.0 copy.65
  194.8 0.1 fusion.11
  194.9 0.1 fusion.6
  195.1 0.5 fusion.7
  195.6 1.8 fusion.40
  197.4 1.6 copy.63
  199.1 86.2 %reduce-scatter.5.cloned.1.call-done = f32[160,128]{1,0:T(8,128)} async-done(((f32[3840,128]{1,0:T(8,128)}), f32[160,128]{1,0:T(8,128)}) %reduce-scatter.5.cloned.1.call-update) | async-done | bytes 81936 | tf_op jit(solution)/shard_map/reduce_scatter | solution.py:139
  285.3 1.5 convert_element_type.47
  (45 shorter events, 1.6 us)
Async XLA Ops:
  6.5 9.4 %copy-start = (bf16[128,4096]{1,0:T(8,128)(2,1)S(1)}, bf16[128,4096]{1,0:T(8,128)(2,1)}, u32[]{:S(2)}) copy-start(bf16[128,4096]{1,0:T(8,128)(2,1)} %param.11) | copy-start | bytes 3145732
  6.5 10.9 %copy-start.5 = (f32[2]{0:T(128)S(1)}, f32[2]{0:T(128)}, u32[]{:S(2)}) copy-start(f32[2]{0:T(128)} %constant.147.clone) | copy-start | bytes 28
  6.5 10.9 %copy-start.3 = (s32[4096]{0:T(1024)S(1)}, s32[4096]{0:T(1024)}, u32[]{:S(2)}) copy-start(s32[4096]{0:T(1024)} %param.19) | copy-start | bytes 49156
  6.5 39.0 %copy-start.1 = (bf16[4096,128]{1,0:T(8,128)(2,1)S(1)}, bf16[4096,128]{1,0:T(8,128)(2,1)}, u32[]{:S(2)}) copy-start(bf16[4096,128]{1,0:T(8,128)(2,1)} %param.12) | copy-start | bytes 3145732
  19.4 29.7 %all-to-all-start.1 = ((bf16[32,5,32]{2,1,0:T(8,128)(2,1)}), bf16[32,5,32]{2,1,0:T(8,128)(2,1)S(1)}, u32[]{:S(2)}, u32[]{:S(2)}) async-start(bf16[32,5,32]{2,1,0:T(8,128)(2,1)} %all_to_all.27), calls=%async_computation.1 | async-start | bytes 131072 | tf_op jit(solution)/shard_map/all_to_all | solution.py:77
  49.1 45.9 %all-to-all-start = ((bf16[32,5,128]{2,1,0:T(8,128)(2,1)}), bf16[32,5,128]{2,1,0:T(8,128)(2,1)S(1)}, u32[]{:S(2)}, u32[]{:S(2)}) async-start(bf16[32,5,128]{2,1,0:T(8,128)(2,1)} %all_to_all.24), calls=%async_computation | async-start | bytes 131072 | tf_op jit(solution)/shard_map/all_to_all | solution.py:76
  58.3 135.4 %reduce-scatter.7.cloned.1.call-start = ((), (), s32[]{:S(2)}) async-start(), calls=%async_computation.6 | async-start | bytes 4096000
  108.7 0.9 copy-start.2
  108.7 12.6 %copy-start.4 = (s32[128]{0:T(128)S(1)}, s32[128]{0:T(128)}, u32[]{:S(2)}) copy-start(s32[128]{0:T(128)} %param.18) | copy-start | bytes 1540
  111.8 18.4 %all-to-all-start.2 = ((bf16[32,5,32]{2,1,0:T(8,128)(2,1)}), bf16[32,5,32]{2,1,0:T(8,128)(2,1)S(1)}, u32[]{:S(2)}, u32[]{:S(2)}) async-start(bf16[32,5,32]{2,1,0:T(8,128)(2,1)} %all_to_all.30), calls=%async_computation.2 | async-start | bytes 131072 | tf_op jit(solution)/shard_map/all_to_all | solution.py:78
  121.3 164.0 %reduce-scatter.5.cloned.1.call-start = ((), (), s32[]{:S(2)}) async-start(), calls=%async_computation.5 | async-start | bytes 2048000 | tf_op jit(solution)/shard_map/reduce_scatter | solution.py:139
Sparse Core Ops, SparseCore 0:
  108.9 84.8 reduce-scatter.6
  199.2 86.0 reduce-scatter.4
where the time goes:
time: 296 us; the launch traced here: 294 us
  waiting for transfers between devices  133 us (45%)
  blocking collectives  58.7 us (20%)
  local copies, waits for them, and re-layouts  40.8 us (14%)
  starting transfers between devices  29.3 us (10%)
  between operations  13.7 us (5%)
  other arithmetic  12.8 us (4%)
  matrix products  4.77 us (2%)
    reduce_scatter x1, waiting for transfers between devices, on_device(): lax.psum_scatter(jnp.einsum('kg,tgd->ktd', chooser, spread, precision=hig...  86.2 us
    unnamed x3, waiting for transfers between devices  39.4 us
    all_gather x1, blocking collectives, on_device(): lax.all_gather(key_slots, 'mp', axis=1, tiled=True)  35.5 us
    all_gather x1, blocking collectives, on_device(): lax.all_gather(value_slots, 'mp', axis=1, tiled=True)  23.2 us
    scatter x1, local copies, waits for them, and re-layouts, on_device(): slot_of = jnp.full((seq_count * send_cap,), capacity, jnp.int32).at[recv_...  15.5 us
    all_to_all x1, starting transfers between devices, on_device(): lax.all_to_all(outgoing_k, 'seq', split_axis=0, concat_axis=0, tiled=True)  10.5 us
    all_to_all x1, starting transfers between devices, on_device(): lax.all_to_all(outgoing_v, 'seq', split_axis=0, concat_axis=0, tiled=True)  9.49 us
    all_to_all x1, starting transfers between devices, on_device(): lax.all_to_all(outgoing_q, 'seq', split_axis=0, concat_axis=0, tiled=True)  9.23 us
  transfers between devices with their start and end apart: 5, of which 3 were waited for; matrix products, arithmetic and copies ran while one was open for 8% of the time, Pallas kernels for 0%

commit v1 on v0

v1 whole, which is shorter than its diff:
```python
import functools

import jax
import jax.numpy as jnp
import numpy as np
from jax import lax
from jax.experimental import pallas as pl
from jax.experimental.pallas import tpu as pltpu
from jax.sharding import Mesh
from jax.sharding import PartitionSpec as P

THETA = 500000.0
N_SEQ = 32
HEADS = 24
GROUP = 4
HEAD_DIM = 128
KV_COLS = 32
TOK = 128
CAP = 160
PIECE = 8
META = 5
SHORT = 16
F32 = jnp.float32
BF16 = jnp.bfloat16


def iota(shape, dim):
    return lax.broadcasted_iota(jnp.int32, shape, dim)


def dot_nt(a, b):
    return lax.dot_general(a, b, (((1,), (1,)), ((), ())), preferred_element_type=F32)


def dot_nn(a, b):
    return lax.dot_general(a, b, (((1,), (0,)), ((), ())), preferred_element_type=F32)


def project_kernel(
    steps, hid, wq, wk, wv, lens, own, order, freq, send, info, acc_q, acc_kv, cos_t, sin_t, place, meta
):
    step = pl.program_id(0)
    sub = lax.axis_index("sub")

    @pl.when(step == 0)
    def _():
        shape = (TOK, TOK)
        row, col = iota(shape, 0), iota(shape, 1)
        eye = row == col
        low = row < col

        def down(value):
            return jnp.sum(jnp.where(eye, value, 0.0), axis=1, keepdims=True)

        def across(value):
            return jnp.sum(jnp.where(eye, value, 0.0), axis=0, keepdims=True)

        len_row = lens[...].astype(F32)
        own_row = own[...].astype(F32)
        len_col, own_col = down(len_row), down(own_row)
        start = jnp.sum(jnp.where(low, len_col, 0.0), axis=0, keepdims=True)
        shard_start = jnp.sum(
            jnp.where(low & (own_col == own_row), len_col, 0.0), axis=0, keepdims=True
        )
        info[...] = jnp.broadcast_to(shard_start, (8, TOK))
        packed = down(order[pl.ds(lax.axis_index("seq"), 1), :].astype(F32))
        inside = (packed >= start) & (packed < start + len_row)

        def pick(value):
            return jnp.sum(jnp.where(inside, value, 0.0), axis=1, keepdims=True)

        target = pick(own_row)
        position = packed - pick(start)
        slot = pick(shard_start) + position
        target_row = across(target)
        rank = jnp.sum(
            jnp.where((target_row == target) & (col < row), 1.0, 0.0), axis=1, keepdims=True
        )
        send_row = across(target * PIECE + rank)
        angle = position * freq[...]
        cos_t[...] = jnp.cos(angle)
        sin_t[...] = jnp.sin(angle)
        rows = iota((N_SEQ * PIECE, TOK), 0).astype(F32)
        place[:, :TOK] = jnp.where(rows == send_row, 1.0, 0.0).astype(BF16)
        place[:, TOK:] = jnp.where(rows == target_row * PIECE + META, 1.0, 0.0).astype(BF16)
        meta[...] = jnp.where(col.astype(F32) == rank, slot + 1.0, 0.0).astype(BF16)
        acc_q[...] = jnp.zeros_like(acc_q)
        acc_kv[...] = jnp.zeros_like(acc_kv)

    block = hid[...]
    acc_q[...] += dot_nn(block, wq[...])
    zero = jnp.zeros_like(wk[...])
    acc_kv[...] += dot_nt(block, jnp.concatenate([wk[...], zero, wv[...], zero], axis=0))

    @pl.when(step == steps - 1)
    def _():
        lane = iota((TOK, HEAD_DIM), 1)
        even = lane % 2 == 0
        cos_a, sin_a = cos_t[...], sin_t[...]

        def rope(value):
            partner = jnp.where(
                even, -pltpu.roll(value, HEAD_DIM - 1, 1), pltpu.roll(value, 1, 1)
            )
            return value * cos_a + partner * sin_a

        query = rope(acc_q[...]).astype(BF16)
        kv = pltpu.roll(acc_kv[...], KV_COLS * sub, 1)
        kv = jnp.where(lane // KV_COLS == sub, rope(kv), kv).astype(BF16)
        spots = place[...]
        send[:, :HEAD_DIM] = dot_nn(spots, jnp.concatenate([query, meta[...]], axis=0)).astype(BF16)
        send[:, HEAD_DIM:] = dot_nn(spots[:, :TOK], kv).astype(BF16)


def logits_kernel(scale, got, gathered, out, values):
    rows = N_SEQ * PIECE
    head = got[...].astype(F32).reshape(N_SEQ, PIECE, HEAD_DIM)
    tags = jnp.broadcast_to(head[:, META : META + 1, :], head.shape)
    hit = iota(head.shape, 2) == iota(head.shape, 1)
    slot_col = jnp.sum(jnp.where(hit, tags, 0.0), axis=2, keepdims=True).reshape(rows, 1) - 1.0
    same = iota((rows, rows), 0) == iota((rows, rows), 1)
    slot_row = jnp.sum(jnp.where(same, slot_col, 0.0), axis=0, keepdims=True)

    window = iota((rows, HEAD_DIM), 1) // KV_COLS
    key = jnp.zeros((rows, HEAD_DIM), F32)
    value = jnp.zeros((rows, HEAD_DIM), F32)
    for c in range(GROUP):
        tile = gathered[c * rows : (c + 1) * rows, :].astype(F32)
        key = jnp.where(window == c, tile, key)
        value = jnp.where(window == (c + 2) % GROUP, tile, value)
    value = pltpu.roll(value, HEAD_DIM // 2, 1)

    n = iota((rows, 1), 0)
    kv_slot = jnp.where(n < 128, n, 128 + n % 32).astype(F32)
    kv_spots = jnp.where(kv_slot == slot_row, 1.0, 0.0).astype(BF16)
    n = iota((224, 1), 0)
    late = jnp.where(n % 8 < 4, 64 + n // 8 * 4 + n % 8, -5)
    strided = 128 + 4 * (n % 8) + (n - 192) // 8
    q_slot = jnp.where(n < 128, n, jnp.where(n < 192, late, strided)).astype(F32)
    q_spots = jnp.where(q_slot == slot_row, 1.0, 0.0).astype(BF16)
    query = dot_nn(q_spots, got[...]).astype(BF16)
    key = dot_nn(kv_spots, key.astype(BF16)).astype(BF16)
    values[...] = dot_nn(kv_spots, value.astype(BF16)).astype(BF16)

    main = dot_nt(query[:192], key[:128]) * scale
    tail = dot_nt(query[192:], key[128:]) * scale
    lane = iota((8, HEAD_DIM), 1) // 32
    packed = jnp.zeros((8, HEAD_DIM), F32)
    for j in range(4):
        packed = jnp.where(lane == j, tail[8 * j : 8 * j + 8], packed)
    out[:SHORT] = main[:128].reshape(SHORT, 8, 128)
    long = main[128:].reshape(8, 8, 128)
    fifth = iota(long.shape, 1) == 4
    out[SHORT:] = jnp.where(fifth, jnp.broadcast_to(packed[:, None, :], long.shape), long)


def mix(coefs, terms, transpose):
    sums = []
    for j in range(HEADS):
        total = coefs[0, j] * terms[0]
        for h in range(1, HEADS):
            total = total + coefs[h, j] * terms[h]
        sums.append(total)
    return jnp.stack(sums)


def soften_kernel(logits, before, after, lens, own, info, out):
    owner = lax.axis_index("grp") * GROUP + lax.axis_index("sub")
    shard = lax.axis_index("seq")
    is_long = owner >= SHORT
    line = iota((8, 128), 0)
    lane = iota((8, 128), 1)
    slot = jnp.where(is_long, 128 + 4 * (owner - SHORT), 8 * owner) + line
    valid = jnp.logical_or(line < 4, jnp.logical_not(is_long))
    begin = info[...]
    length = lens[...].astype(F32)
    slot_f = slot.astype(F32)
    held = (own[...] == shard) & (slot_f >= begin) & (slot_f < begin + length) & valid
    filled = jnp.sum(jnp.where(held, 1.0, 0.0), axis=1, keepdims=True) > 0.5
    first = jnp.sum(jnp.where(held, begin, 0.0), axis=1, keepdims=True)

    def allowed(other):
        other_f = other.astype(F32)
        return (other_f >= first) & (other_f <= slot_f) & filled

    main_ok = allowed(lane)
    tail_ok = allowed(128 + lane % 32) & is_long & (lane // 32 == line)
    mixed = mix(before, [logits[h] for h in range(HEADS)], False)
    tail = jnp.broadcast_to(mixed[:, 4:5, :], mixed.shape)
    main_m = jnp.where(main_ok[None], mixed, -1e30)
    tail_m = jnp.where(tail_ok[None], tail, -1e30)
    top = jnp.max(jnp.maximum(main_m, tail_m), axis=2, keepdims=True)
    main_e = jnp.where(main_ok[None], jnp.exp(main_m - top), 0.0)
    tail_e = jnp.where(tail_ok[None], jnp.exp(tail_m - top), 0.0)
    total = jnp.sum(main_e + tail_e, axis=2, keepdims=True)
    total = jnp.where(filled[None], total, 1.0)
    main_w = (main_e / total).astype(BF16).astype(F32)
    tail_w = (tail_e / total).astype(BF16).astype(F32)
    tail_w = jnp.broadcast_to(jnp.sum(tail_w, axis=1, keepdims=True), tail_w.shape)
    weights = jnp.where(((line == 4) & is_long)[None], tail_w, main_w)
    out[...] = mix(after, [weights[h] for h in range(HEADS)], True).astype(BF16)


def output_kernel(weights, values, out):
    out[:128, :] = dot_nn(weights[:128, :], values[:128, :]).astype(BF16)
    long = weights[128:, :].astype(F32).reshape(8, 8, 128)
    tail = jnp.broadcast_to(long[:, 4:5, :], long.shape)
    tail = jnp.where(iota(long.shape, 2) // 32 == iota(long.shape, 1), tail, 0.0)
    rows = dot_nn(weights[128:, :], values[:128, :]) + dot_nn(
        tail.reshape(64, 128).astype(BF16), values[128:, :]
    )
    for i in range(8):
        out[128 + 4 * i : 132 + 4 * i, :] = rows[8 * i : 8 * i + 4, :].astype(BF16)


def on_device(
    hidden, w_query, w_key, w_value, mix_before, mix_after, doc_lengths, doc_owner, loader_order
):
    depth = hidden.shape[1]
    steps = 4
    part = depth // steps
    rows = N_SEQ * PIECE
    vmem = pl.BlockSpec(memory_space=pltpu.VMEM)
    smem = pl.BlockSpec(memory_space=pltpu.SMEM)
    pair = np.arange(HEAD_DIM) // 2
    freq = jnp.asarray((THETA ** (-2.0 * pair / HEAD_DIM)).astype(np.float32)[None, :])
    lens = doc_lengths.reshape(1, TOK)
    own = doc_owner.reshape(1, TOK)
    order = loader_order.reshape(N_SEQ, TOK)

    def whole(shape):
        return pl.BlockSpec(shape, lambda k: (0, 0))

    send, info = pl.pallas_call(
        functools.partial(project_kernel, steps),
        grid=(steps,),
        in_specs=[
            pl.BlockSpec((TOK, part), lambda k: (0, k)),
            pl.BlockSpec((part, HEAD_DIM), lambda k: (k, 0)),
            pl.BlockSpec((KV_COLS, part), lambda k: (0, k)),
            pl.BlockSpec((KV_COLS, part), lambda k: (0, k)),
            whole((1, TOK)),
            whole((1, TOK)),
            whole((N_SEQ, TOK)),
            whole((1, TOK)),
        ],
        out_specs=[whole((rows, 2 * HEAD_DIM)), whole((8, TOK))],
        out_shape=[
            jax.ShapeDtypeStruct((rows, 2 * HEAD_DIM), BF16),
            jax.ShapeDtypeStruct((8, TOK), F32),
        ],
        scratch_shapes=[
            pltpu.VMEM((TOK, HEAD_DIM), F32),
            pltpu.VMEM((TOK, HEAD_DIM), F32),
            pltpu.VMEM((TOK, HEAD_DIM), F32),
            pltpu.VMEM((TOK, HEAD_DIM), F32),
            pltpu.VMEM((rows, 2 * TOK), BF16),
            pltpu.VMEM((TOK, TOK), BF16),
        ],
        name="project",
    )(hidden, w_query, w_key.T, w_value.T, lens, own, order, freq)

    got = lax.all_to_all(
        send.reshape(N_SEQ, PIECE, 2 * HEAD_DIM), "seq", split_axis=0, concat_axis=0, tiled=True
    ).reshape(rows, 2 * HEAD_DIM)
    gathered = lax.all_gather(got[:, HEAD_DIM:], "sub", axis=0, tiled=True)

    logits, values = pl.pallas_call(
        functools.partial(logits_kernel, 1.0 / HEAD_DIM**0.5),
        in_specs=[vmem, vmem],
        out_specs=[vmem, vmem],
        out_shape=[
            jax.ShapeDtypeStruct((HEADS, 8, 128), F32),
            jax.ShapeDtypeStruct((rows, HEAD_DIM), BF16),
        ],
        name="logits",
    )(got[:, :HEAD_DIM], gathered)

    mine = lax.all_to_all(logits, ("grp", "sub"), split_axis=0, concat_axis=0, tiled=True)
    blended = pl.pallas_call(
        soften_kernel,
        in_specs=[vmem, smem, smem, vmem, vmem, vmem],
        out_specs=vmem,
        out_shape=jax.ShapeDtypeStruct((HEADS, 8, 128), BF16),
        name="soften",
    )(mine, mix_before, mix_after, lens, own, info)
    back = lax.all_to_all(blended, ("grp", "sub"), split_axis=0, concat_axis=0, tiled=True)
    return pl.pallas_call(
        output_kernel,
        in_specs=[vmem, vmem],
        out_specs=vmem,
        out_shape=jax.ShapeDtypeStruct((CAP, HEAD_DIM), BF16),
        name="output",
    )(back.reshape(HEADS * 8, 128), values)


def solution(mesh):
    split = Mesh(
        mesh.devices.reshape(N_SEQ, HEADS // GROUP, GROUP), ("seq", "grp", "sub")
    ) if not isinstance(mesh, jax.sharding.AbstractMesh) else mesh
    mp = ("grp", "sub")
    placed = (P("seq", None), P(None, mp), P(None, mp), P(None, mp), P(), P(), P(), P(), P())
    return jax.shard_map(
        on_device, mesh=split, in_specs=placed, out_specs=P("seq", mp), check_vma=False
    )
```

time: 296 us -> 81.4 us (0.28)
  waiting for transfers between devices: 133 us -> 0 us
  local copies, waits for them, and re-layouts: 40.8 us -> 0.63 us
  starting transfers between devices: 29.3 us -> 0 us
  between operations: 13.7 us -> 0.01 us
  other arithmetic: 12.8 us -> 0 us
  Pallas kernels: 0 us -> 10.8 us
  blocking collectives: 58.7 us -> 69.5 us
  matrix products: 4.77 us -> 0 us
    reduce_scatter x1 -> x0, waiting for transfers between devices: 86.2 us -> none  [on_device(): lax.psum_scatter(jnp.einsum('kg,tgd->ktd', chooser, spread, precision=hig...]
    all_to_all x0 -> x3, blocking collectives: none -> 58.5 us  [the longest x1 23.5 us: on_device(): lax.all_to_all(logits, ('grp', 'sub'), split_axis=0, concat_axis=0, tiled...]
    all_gather x2 -> x1, blocking collectives: 58.7 us -> 11.1 us  [on_device(): gathered = lax.all_gather(got[:, HEAD_DIM:], 'sub', axis=0, tiled=True)]
    unnamed x3 -> x0, waiting for transfers between devices: 39.4 us -> none
    all_to_all x3 -> x0, starting transfers between devices: 29.2 us -> none  [the longest x1 10.5 us: on_device(): lax.all_to_all(outgoing_k, 'seq', split_axis=0, concat_axis=0, tiled=True)]
    scatter x9 -> x0, local copies, waits for them, and re-layouts: 21.3 us -> none  [the longest x1 15.5 us: on_device(): slot_of = jnp.full((seq_count * send_cap,), capacity, jnp.int32).at[recv_...]
    pallas_call x0 -> x4, Pallas kernels: none -> 10.8 us  [the longest x1 4.61 us: on_device(): pl.pallas_call(functools.partial(project_kernel, steps), grid=(steps,), i...]
    all_to_all x3 -> x0, waiting for transfers between devices: 7.83 us -> none  [the longest x1 7.82 us: on_device(): lax.all_to_all(outgoing_v, 'seq', split_axis=0, concat_axis=0, tiled=True)]
  transfers between devices with their start and end apart: 5 -> 0, of which waited for: 3 -> 0; matrix products, arithmetic and copies ran while one was open for 8% -> 0% of each run, Pallas kernels for 0% -> 0%
where the time goes in v1:
time: 81.4 us; the launch traced here: 81 us
  blocking collectives  69.5 us (85%)
  Pallas kernels  10.8 us (13%)
    all_to_all x1, blocking collectives, on_device(): lax.all_to_all(logits, ('grp', 'sub'), split_axis=0, concat_axis=0, tiled...  23.5 us
    all_to_all x1, blocking collectives, on_device(): lax.all_to_all(send.reshape(N_SEQ, PIECE, 2 * HEAD_DIM), 'seq', split_axi...  19.8 us
    all_to_all x1, blocking collectives, on_device(): lax.all_to_all(blended, ('grp', 'sub'), split_axis=0, concat_axis=0, tile...  15.1 us
    all_gather x1, blocking collectives, on_device(): gathered = lax.all_gather(got[:, HEAD_DIM:], 'sub', axis=0, tiled=True)  11.1 us
    pallas_call x1, Pallas kernels, on_device(): pl.pallas_call(functools.partial(project_kernel, steps), grid=(steps,), i...  4.61 us
    pallas_call x1, Pallas kernels, on_device(): pl.pallas_call(soften_kernel, in_specs=[vmem, smem, smem, vmem, vmem, vme...  2.44 us
    pallas_call x1, Pallas kernels, on_device(): pl.pallas_call(functools.partial(logits_kernel, 1.0 / HEAD_DIM ** 0.5), i...  2.1 us
    pallas_call x1, Pallas kernels, on_device(): pl.pallas_call(output_kernel, in_specs=[vmem, vmem], out_specs=vmem, out_...  1.65 us

profile of v1, /device:TPU:1, one launch (start us, length us, event | category | flops | bytes accessed | tf_op | source)
XLA Modules:
  0.0 81.0 jit_solution(992151049836605640)
XLA Ops:
  0.0 4.6 %project.1 = (bf16[256,256]{1,0:T(8,128)(2,1)}, f32[8,128]{1,0:T(8,128)}) custom-call(bf16[128,4096]{1,0:T(8,128)(2,1)} %hid.1, bf16[4096,128]{1,0:T(8,128)(2,1)} %wq.1, bf16[32,4096]{1,0:T(8,128)(2,1)} %bitcast.9, bf16[32,4096]{1,0:T(8,128)(2,1)} %bitcast.10, s32[1,128]{1,0:T(1,128)} %bitcast.14, s32[1,128]{1,0:T(1,128)} %bitcast.16, s32[32,128]{1,0:T(8,128)} %bitcast.13, ...), custom_call_target="tpu_custom_call" | custom-call | tf_op jit(solution)/shard_map/project/pallas_call | solution.py:234
  4.6 19.8 %all_to_all.15 = bf16[32,8,256]{2,1,0:T(8,128)(2,1)S(1)} all-to-all(bf16[32,8,256]{2,1,0:T(8,128)(2,1)} %bitcast.12), channel_id=1, replica_groups=mesh['seq'=32,'grp'=6,'sub'=4] {'seq'}, dimensions={0} | all-to-all | bytes 262144 | tf_op jit(solution)/shard_map/all_to_all | solution.py:263
  24.4 0.6 fusion
  25.1 11.1 %all_gather.3.gathered = bf16[1024,128]{1,0:T(8,128)(2,1)} all-gather(bf16[256,128]{1,0:T(8,128)(2,1)S(1)} %get-tuple-element.13), channel_id=1, replica_groups=mesh['seq'=32,'grp'=6,'sub'=4] {'sub'}, dimensions={0}, use_global_device_ids=true | all-gather | bytes 327680 | tf_op jit(solution)/shard_map/all_gather | solution.py:266
  36.2 2.1 %logits.1 = (f32[24,8,128]{2,1,0:T(8,128)}, bf16[256,128]{1,0:T(8,128)(2,1)}) custom-call(bf16[256,128]{1,0:T(8,128)(2,1)} %get-tuple-element.14.got, bf16[1024,128]{1,0:T(8,128)(2,1)} %all_gather.3.gathered), custom_call_target="tpu_custom_call" | custom-call | tf_op jit(solution)/shard_map/logits/pallas_call | solution.py:268
  38.3 23.5 %all_to_all.16.logits = f32[24,8,128]{2,1,0:T(8,128)} all-to-all(f32[24,8,128]{2,1,0:T(8,128)} %get-tuple-element.10), channel_id=1, replica_groups=mesh['seq'=32,'grp'=6,'sub'=4] {'grp','sub'}, dimensions={0} | all-to-all | bytes 196608 | tf_op jit(solution)/shard_map/all_to_all | solution.py:279
  61.8 2.4 %soften.1 = bf16[24,8,128]{2,1,0:T(8,128)(2,1)} custom-call(f32[24,8,128]{2,1,0:T(8,128)} %all_to_all.16.logits, f32[24,24]{1,0:T(8,128)} %before.1, f32[24,24]{1,0:T(8,128)} %after.1, s32[1,128]{1,0:T(1,128)} %bitcast.15, s32[1,128]{1,0:T(1,128)} %bitcast.17, f32[8,128]{1,0:T(8,128)} %get-tuple-element.11.info), custom_call_target="tpu_custom_call" | custom-call | tf_op jit(solution)/shard_map/soften/pallas_call | solution.py:280
  64.2 15.1 %all_to_all.17 = bf16[24,8,128]{2,1,0:T(8,128)(2,1)} all-to-all(bf16[24,8,128]{2,1,0:T(8,128)(2,1)} %soften.1), channel_id=1, replica_groups=mesh['seq'=32,'grp'=6,'sub'=4] {'grp','sub'}, dimensions={0} | all-to-all | bytes 98304 | tf_op jit(solution)/shard_map/all_to_all | solution.py:287
  79.3 1.6 %output.1 = bf16[160,128]{1,0:T(8,128)(2,1)} custom-call(bf16[192,128]{1,0:T(8,128)(2,1)} %bitcast.11, bf16[256,128]{1,0:T(8,128)(2,1)} %get-tuple-element.12.values), custom_call_target="tpu_custom_call" | custom-call | tf_op jit(solution)/shard_map/output/pallas_call | solution.py:288

commit v2 on v1

v2 whole, which is shorter than its diff:
```python
import functools

import jax
import jax.numpy as jnp
import numpy as np
from jax import lax
from jax.experimental import pallas as pl
from jax.experimental.pallas import tpu as pltpu
from jax.sharding import Mesh
from jax.sharding import PartitionSpec as P

THETA = 500000.0
N_SEQ = 32
HEADS = 24
GROUP = 4
HEAD_DIM = 128
KV_COLS = 32
TOK = 128
CAP = 160
PIECE = 8
META = 5
SHORT = 16
F32 = jnp.float32
BF16 = jnp.bfloat16
PARTS = 4


def iota(shape, dim):
    return lax.broadcasted_iota(jnp.int32, shape, dim)


def dot_nt(a, b):
    return lax.dot_general(a, b, (((1,), (1,)), ((), ())), preferred_element_type=F32)


def dot_nn(a, b):
    return lax.dot_general(a, b, (((1,), (0,)), ((), ())), preferred_element_type=F32)


def project_kernel(
    hid_h, wq_h, wk_h, wv_h, lens_h, own_h, order_h, freq_h, send, info,
    hid, wq, wkv, lens, own, order, freq, cos_t, sin_t, place, sems,
):
    sub = lax.axis_index("sub")
    part = hid.shape[1] // PARTS
    copies = []

    def copy(source, target):
        copies.append(pltpu.make_async_copy(source, target, sems.at[len(copies)]))
        copies[-1].start()

    copy(lens_h, lens)
    copy(own_h, own)
    copy(order_h, order)
    copy(freq_h, freq)
    for k in range(PARTS):
        span = pl.ds(k * part, part)
        copy(hid_h.at[:, span], hid.at[:, span])
        copy(wq_h.at[span, :], wq.at[span, :])
        copy(wk_h.at[:, span], wkv.at[pl.ds(0, KV_COLS), span])
        copy(wv_h.at[:, span], wkv.at[pl.ds(2 * KV_COLS, KV_COLS), span])
    blank = jnp.zeros((KV_COLS, hid.shape[1]), BF16)
    wkv[KV_COLS : 2 * KV_COLS, :] = blank
    wkv[3 * KV_COLS :, :] = blank
    for k in range(4):
        copies[k].wait()

    shape = (TOK, TOK)
    row, col = iota(shape, 0), iota(shape, 1)
    eye = row == col
    low = row < col

    def down(value):
        return jnp.sum(jnp.where(eye, value, 0.0), axis=1, keepdims=True)

    def across(value):
        return jnp.sum(jnp.where(eye, value, 0.0), axis=0, keepdims=True)

    len_row = lens[...].astype(F32)
    own_row = own[...].astype(F32)
    len_col, own_col = down(len_row), down(own_row)
    start = jnp.sum(jnp.where(low, len_col, 0.0), axis=0, keepdims=True)
    shard_start = jnp.sum(
        jnp.where(low & (own_col == own_row), len_col, 0.0), axis=0, keepdims=True
    )
    info[...] = jnp.broadcast_to(shard_start, (8, TOK))
    packed = down(order[pl.ds(lax.axis_index("seq"), 1), :].astype(F32))
    inside = (packed >= start) & (packed < start + len_row)

    def pick(value):
        return jnp.sum(jnp.where(inside, value, 0.0), axis=1, keepdims=True)

    target = pick(own_row)
    position = packed - pick(start)
    slot = pick(shard_start) + position
    target_row = across(target)
    rank = jnp.sum(
        jnp.where((target_row == target) & (col < row), 1.0, 0.0), axis=1, keepdims=True
    )
    send_row = across(target * PIECE + rank)
    angle = position * freq[...]
    cos_t[...] = jnp.cos(angle)
    sin_t[...] = jnp.sin(angle)
    rows = iota((N_SEQ * PIECE, TOK), 0).astype(F32)
    place[:, :TOK] = jnp.where(rows == send_row, 1.0, 0.0).astype(BF16)
    place[:, TOK:] = jnp.where(rows == target_row * PIECE + META, 1.0, 0.0).astype(BF16)
    meta = jnp.where(col.astype(F32) == rank, slot + 1.0, 0.0).astype(BF16)

    acc_q = jnp.zeros((TOK, HEAD_DIM), F32)
    acc_kv = jnp.zeros((TOK, HEAD_DIM), F32)
    for k in range(PARTS):
        for c in copies[4 + 4 * k : 8 + 4 * k]:
            c.wait()
        block = hid[:, k * part : (k + 1) * part]
        acc_q = acc_q + dot_nn(block, wq[k * part : (k + 1) * part, :])
        acc_kv = acc_kv + dot_nt(block, wkv[:, k * part : (k + 1) * part])

    even = col % 2 == 0
    cos_a, sin_a = cos_t[...], sin_t[...]

    def rope(value):
        partner = jnp.where(even, -pltpu.roll(value, HEAD_DIM - 1, 1), pltpu.roll(value, 1, 1))
        return value * cos_a + partner * sin_a

    query = rope(acc_q).astype(BF16)
    kv = pltpu.roll(acc_kv, KV_COLS * sub, 1)
    kv = jnp.where(col // KV_COLS == sub, rope(kv), kv).astype(BF16)
    spots = place[...]
    send[:, :HEAD_DIM] = dot_nn(spots, jnp.concatenate([query, meta], axis=0)).astype(BF16)
    send[:, HEAD_DIM:] = dot_nn(spots[:, :TOK], kv).astype(BF16)


def logits_kernel(scale, got, gathered, out, values):
    rows = N_SEQ * PIECE
    mine = got[:, :HEAD_DIM]
    head = mine.astype(F32).reshape(N_SEQ, PIECE, HEAD_DIM)
    tags = jnp.broadcast_to(head[:, META : META + 1, :], head.shape)
    hit = iota(head.shape, 2) == iota(head.shape, 1)
    slot_col = jnp.sum(jnp.where(hit, tags, 0.0), axis=2, keepdims=True).reshape(rows, 1) - 1.0
    same = iota((rows, rows), 0) == iota((rows, rows), 1)
    slot_row = jnp.sum(jnp.where(same, slot_col, 0.0), axis=0, keepdims=True)

    window = iota((rows, HEAD_DIM), 1) // KV_COLS
    key = jnp.zeros((rows, HEAD_DIM), F32)
    value = jnp.zeros((rows, HEAD_DIM), F32)
    for c in range(GROUP):
        tile = gathered[c * rows : (c + 1) * rows, :].astype(F32)
        key = jnp.where(window == c, tile, key)
        value = jnp.where(window == (c + 2) % GROUP, tile, value)
    value = pltpu.roll(value, HEAD_DIM // 2, 1)

    n = iota((rows, 1), 0)
    kv_slot = jnp.where(n < 128, n, 128 + n % 32).astype(F32)
    kv_spots = jnp.where(kv_slot == slot_row, 1.0, 0.0).astype(BF16)
    n = iota((224, 1), 0)
    late = jnp.where(n % 8 < 4, 64 + n // 8 * 4 + n % 8, -5)
    strided = 128 + 4 * (n % 8) + (n - 192) // 8
    q_slot = jnp.where(n < 128, n, jnp.where(n < 192, late, strided)).astype(F32)
    q_spots = jnp.where(q_slot == slot_row, 1.0, 0.0).astype(BF16)
    query = dot_nn(q_spots, mine).astype(BF16)
    key = dot_nn(kv_spots, key.astype(BF16)).astype(BF16)
    values[...] = dot_nn(kv_spots, value.astype(BF16)).astype(BF16)

    main = dot_nt(query[:192], key[:128]) * scale
    tail = dot_nt(query[192:], key[128:]) * scale
    lane = iota((8, HEAD_DIM), 1) // 32
    packed = jnp.zeros((8, HEAD_DIM), F32)
    for j in range(4):
        packed = jnp.where(lane == j, tail[8 * j : 8 * j + 8], packed)
    out[:SHORT] = main[:128].reshape(SHORT, 8, 128)
    long = main[128:].reshape(8, 8, 128)
    fifth = iota(long.shape, 1) == 4
    out[SHORT:] = jnp.where(fifth, jnp.broadcast_to(packed[:, None, :], long.shape), long)


def mix(coefs, terms):
    sums = []
    for j in range(HEADS):
        total = coefs[0, j] * terms[0]
        for h in range(1, HEADS):
            total = total + coefs[h, j] * terms[h]
        sums.append(total)
    return jnp.stack(sums)


def soften_kernel(logits, before, after, lens, own, info, out):
    owner = lax.axis_index("grp") * GROUP + lax.axis_index("sub")
    shard = lax.axis_index("seq")
    is_long = owner >= SHORT
    line = iota((8, 128), 0)
    lane = iota((8, 128), 1)
    slot = jnp.where(is_long, 128 + 4 * (owner - SHORT), 8 * owner) + line
    valid = jnp.logical_or(line < 4, jnp.logical_not(is_long))
    begin = info[...]
    length = lens[...].astype(F32)
    slot_f = slot.astype(F32)
    held = (own[...] == shard) & (slot_f >= begin) & (slot_f < begin + length) & valid
    filled = jnp.sum(jnp.where(held, 1.0, 0.0), axis=1, keepdims=True) > 0.5
    first = jnp.sum(jnp.where(held, begin, 0.0), axis=1, keepdims=True)

    def allowed(other):
        other_f = other.astype(F32)
        return (other_f >= first) & (other_f <= slot_f) & filled

    main_ok = allowed(lane)
    tail_ok = allowed(128 + lane % 32) & is_long & (lane // 32 == line)
    mixed = mix(before, [logits[h] for h in range(HEADS)])
    tail = jnp.broadcast_to(mixed[:, 4:5, :], mixed.shape)
    main_m = jnp.where(main_ok[None], mixed, -1e30)
    tail_m = jnp.where(tail_ok[None], tail, -1e30)
    top = jnp.max(jnp.maximum(main_m, tail_m), axis=2, keepdims=True)
    main_e = jnp.where(main_ok[None], jnp.exp(main_m - top), 0.0)
    tail_e = jnp.where(tail_ok[None], jnp.exp(tail_m - top), 0.0)
    total = jnp.sum(main_e + tail_e, axis=2, keepdims=True)
    total = jnp.where(filled[None], total, 1.0)
    main_w = (main_e / total).astype(BF16).astype(F32)
    tail_w = (tail_e / total).astype(BF16).astype(F32)
    tail_w = jnp.broadcast_to(jnp.sum(tail_w, axis=1, keepdims=True), tail_w.shape)
    weights = jnp.where(((line == 4) & is_long)[None], tail_w, main_w)
    out[...] = mix(after, [weights[h] for h in range(HEADS)]).astype(BF16)


def output_kernel(weights, values, out):
    out[:128, :] = dot_nn(weights[:128, :], values[:128, :]).astype(BF16)
    long = weights[128:, :].astype(F32).reshape(8, 8, 128)
    tail = jnp.broadcast_to(long[:, 4:5, :], long.shape)
    tail = jnp.where(iota(long.shape, 2) // 32 == iota(long.shape, 1), tail, 0.0)
    rows = dot_nn(weights[128:, :], values[:128, :]) + dot_nn(
        tail.reshape(64, 128).astype(BF16), values[128:, :]
    )
    for i in range(8):
        out[128 + 4 * i : 132 + 4 * i, :] = rows[8 * i : 8 * i + 4, :].astype(BF16)


def on_device(
    hidden, w_query, w_key, w_value, mix_before, mix_after, doc_lengths, doc_owner, loader_order
):
    depth = hidden.shape[1]
    grant = pltpu.CompilerParams(vmem_limit_bytes=12 << 20)
    rows = N_SEQ * PIECE
    vmem = pl.BlockSpec(memory_space=pltpu.VMEM)
    smem = pl.BlockSpec(memory_space=pltpu.SMEM)
    pair = np.arange(HEAD_DIM) // 2
    freq = jnp.asarray((THETA ** (-2.0 * pair / HEAD_DIM)).astype(np.float32)[None, :])
    lens = doc_lengths.reshape(1, TOK)
    own = doc_owner.reshape(1, TOK)
    order = loader_order.reshape(N_SEQ, TOK)

    hbm = pl.BlockSpec(memory_space=pltpu.HBM)
    send, info = pl.pallas_call(
        project_kernel,
        in_specs=[hbm] * 8,
        out_specs=[vmem, vmem],
        out_shape=[
            jax.ShapeDtypeStruct((rows, 2 * HEAD_DIM), BF16),
            jax.ShapeDtypeStruct((8, TOK), F32),
        ],
        scratch_shapes=[
            pltpu.VMEM((TOK, depth), BF16),
            pltpu.VMEM((depth, HEAD_DIM), BF16),
            pltpu.VMEM((4 * KV_COLS, depth), BF16),
            pltpu.VMEM((1, TOK), jnp.int32),
            pltpu.VMEM((1, TOK), jnp.int32),
            pltpu.VMEM((N_SEQ, TOK), jnp.int32),
            pltpu.VMEM((1, TOK), F32),
            pltpu.VMEM((TOK, HEAD_DIM), F32),
            pltpu.VMEM((TOK, HEAD_DIM), F32),
            pltpu.VMEM((rows, 2 * TOK), BF16),
            pltpu.SemaphoreType.DMA((4 + 4 * PARTS,)),
        ],
        compiler_params=grant,
        name="project",
    )(
        *[
            pltpu.with_memory_space_constraint(x, pltpu.HBM)
            for x in (hidden, w_query, w_key.T, w_value.T, lens, own, order, freq)
        ]
    )

    got = lax.all_to_all(
        send.reshape(N_SEQ, PIECE, 2 * HEAD_DIM), "seq", split_axis=0, concat_axis=0, tiled=True
    ).reshape(rows, 2 * HEAD_DIM)
    gathered = lax.all_gather(got[:, HEAD_DIM:], "sub", axis=0, tiled=True)

    logits, values = pl.pallas_call(
        functools.partial(logits_kernel, 1.0 / HEAD_DIM**0.5),
        in_specs=[vmem, vmem],
        out_specs=[vmem, vmem],
        out_shape=[
            jax.ShapeDtypeStruct((HEADS, 8, 128), F32),
            jax.ShapeDtypeStruct((rows, HEAD_DIM), BF16),
        ],
        compiler_params=grant,
        name="logits",
    )(got, gathered)

    mine = lax.all_to_all(logits, ("grp", "sub"), split_axis=0, concat_axis=0, tiled=True)
    blended = pl.pallas_call(
        soften_kernel,
        in_specs=[vmem, smem, smem, vmem, vmem, vmem],
        out_specs=vmem,
        out_shape=jax.ShapeDtypeStruct((HEADS, 8, 128), BF16),
        compiler_params=grant,
        name="soften",
    )(mine, mix_before, mix_after, lens, own, info)
    back = lax.all_to_all(blended, ("grp", "sub"), split_axis=0, concat_axis=0, tiled=True)
    return pl.pallas_call(
        output_kernel,
        in_specs=[vmem, vmem],
        out_specs=vmem,
        out_shape=jax.ShapeDtypeStruct((CAP, HEAD_DIM), BF16),
        compiler_params=grant,
        name="output",
    )(back.reshape(HEADS * 8, 128), values)


def solution(mesh):
    split = Mesh(
        mesh.devices.reshape(N_SEQ, HEADS // GROUP, GROUP), ("seq", "grp", "sub")
    ) if not isinstance(mesh, jax.sharding.AbstractMesh) else mesh
    mp = ("grp", "sub")
    placed = (P("seq", None), P(None, mp), P(None, mp), P(None, mp), P(), P(), P(), P(), P())
    return jax.shard_map(
        on_device, mesh=split, in_specs=placed, out_specs=P("seq", mp), check_vma=False
    )
```

time: 81.4 us -> 73.9 us (0.908)
  Pallas kernels: 10.8 us -> 5.72 us
  blocking collectives: 69.5 us -> 67.2 us
    pallas_call x1, Pallas kernels: 4.61 us -> 2.82 us  [on_device(): pl.pallas_call(project_kernel, in_specs=[hbm] * 8, out_specs=[vmem, vmem]...]
    pallas_call x1, Pallas kernels: 2.1 us -> 0.46 us  [on_device(): pl.pallas_call(functools.partial(logits_kernel, 1.0 / HEAD_DIM ** 0.5), i...]
    all_to_all x1, blocking collectives: 15.1 us -> 13.7 us  [on_device(): lax.all_to_all(blended, ('grp', 'sub'), split_axis=0, concat_axis=0, tile...]
    all_gather x1, blocking collectives: 11.1 us -> 10 us  [on_device(): gathered = lax.all_gather(got[:, HEAD_DIM:], 'sub', axis=0, tiled=True)]
    pallas_call x1, Pallas kernels: 1.65 us -> 0.78 us  [on_device(): pl.pallas_call(output_kernel, in_specs=[vmem, vmem], out_specs=vmem, out_...]
where the time goes in v2:
time: 73.9 us; the launch traced here: 73.6 us
  blocking collectives  67.2 us (91%)
  Pallas kernels  5.72 us (8%)
    all_to_all x1, blocking collectives, on_device(): lax.all_to_all(logits, ('grp', 'sub'), split_axis=0, concat_axis=0, tiled...  23.8 us
    all_to_all x1, blocking collectives, on_device(): lax.all_to_all(send.reshape(N_SEQ, PIECE, 2 * HEAD_DIM), 'seq', split_axi...  19.6 us
    all_to_all x1, blocking collectives, on_device(): lax.all_to_all(blended, ('grp', 'sub'), split_axis=0, concat_axis=0, tile...  13.7 us
    all_gather x1, blocking collectives, on_device(): gathered = lax.all_gather(got[:, HEAD_DIM:], 'sub', axis=0, tiled=True)  10 us
    pallas_call x1, Pallas kernels, on_device(): pl.pallas_call(project_kernel, in_specs=[hbm] * 8, out_specs=[vmem, vmem]...  2.82 us
    pallas_call x1, Pallas kernels, on_device(): pl.pallas_call(soften_kernel, in_specs=[vmem, smem, smem, vmem, vmem, vme...  1.66 us

profile of v2, /device:TPU:1, one launch (start us, length us, event | category | flops | bytes accessed | tf_op | source)
XLA Modules:
  0.0 73.6 jit_solution(16492106916222911567)
XLA Ops:
  0.0 2.8 %project.1 = (bf16[256,256]{1,0:T(8,128)(2,1)S(1)}, f32[8,128]{1,0:T(8,128)S(1)}) custom-call(bf16[128,4096]{1,0:T(8,128)(2,1)} %hid_h.1, bf16[4096,128]{1,0:T(8,128)(2,1)} %wq_h.1, bf16[32,4096]{1,0:T(8,128)(2,1)} %bitcast.16, bf16[32,4096]{1,0:T(8,128)(2,1)} %bitcast.17, s32[1,128]{1,0:T(1,128)} %bitcast.12, s32[1,128]{1,0:T(1,128)} %bitcast.14, ...), custom_call_target="tpu_custom_call" | custom-call | tf_op jit(solution)/shard_map/project/pallas_call | solution.py:250
  2.8 19.6 %all_to_all.15 = bf16[32,8,256]{2,1,0:T(8,128)(2,1)S(1)} all-to-all(bf16[32,8,256]{2,1,0:T(8,128)(2,1)S(1)} %bitcast.11), channel_id=1, replica_groups=mesh['seq'=32,'grp'=6,'sub'=4] {'seq'}, dimensions={0} | all-to-all | bytes 262144 | tf_op jit(solution)/shard_map/all_to_all | solution.py:280
  22.5 10.0 %all_gather.3.gathered = bf16[1024,128]{1,0:T(8,128)(2,1)S(1)} all-gather(bf16[256,128]{1,0:T(8,128)(2,1)S(1)} %slice.4), channel_id=1, replica_groups=mesh['seq'=32,'grp'=6,'sub'=4] {'sub'}, dimensions={0}, use_global_device_ids=true | all-gather | bytes 327680 | tf_op jit(solution)/shard_map/all_gather | solution.py:283
  32.5 0.5 logits.1
  33.0 0.0 copy-start
  33.0 0.0 copy-start.1
  33.0 23.8 %all_to_all.16.logits = f32[24,8,128]{2,1,0:T(8,128)S(1)} all-to-all(f32[24,8,128]{2,1,0:T(8,128)S(1)} %get-tuple-element.10), channel_id=1, replica_groups=mesh['seq'=32,'grp'=6,'sub'=4] {'grp','sub'}, dimensions={0} | all-to-all | bytes 196608 | tf_op jit(solution)/shard_map/all_to_all | solution.py:297
  56.8 0.0 copy-start.2
  56.8 0.0 copy-start.3
  56.8 0.0 copy-done
  56.8 0.0 copy-done.1
  56.8 0.6 copy-done.2
  57.5 0.0 copy-done.3
  57.5 1.7 %soften.1 = bf16[24,8,128]{2,1,0:T(8,128)(2,1)S(1)} custom-call(f32[24,8,128]{2,1,0:T(8,128)S(1)} %all_to_all.16.logits, f32[24,24]{1,0:T(8,128)S(1)} %copy-done, f32[24,24]{1,0:T(8,128)S(1)} %copy-done.1, s32[1,128]{1,0:T(1,128)S(1)} %bitcast.13, s32[1,128]{1,0:T(1,128)S(1)} %bitcast.15, f32[8,128]{1,0:T(8,128)S(1)} %get-tuple-element.11.info), custom_call_target="tpu_custom_call" | custom-call | tf_op jit(solution)/shard_map/soften/pallas_call | solution.py:298
  59.1 13.7 %all_to_all.17 = bf16[24,8,128]{2,1,0:T(8,128)(2,1)S(1)} all-to-all(bf16[24,8,128]{2,1,0:T(8,128)(2,1)S(1)} %soften.1), channel_id=1, replica_groups=mesh['seq'=32,'grp'=6,'sub'=4] {'grp','sub'}, dimensions={0} | all-to-all | bytes 98304 | tf_op jit(solution)/shard_map/all_to_all | solution.py:306
  72.8 0.8 %output.1 = bf16[160,128]{1,0:T(8,128)(2,1)} custom-call(bf16[192,128]{1,0:T(8,128)(2,1)S(1)} %bitcast.10, bf16[256,128]{1,0:T(8,128)(2,1)S(1)} %get-tuple-element.12.values), custom_call_target="tpu_custom_call" | custom-call | tf_op jit(solution)/shard_map/output/pallas_call | solution.py:307
  (1 shorter events, 0.0 us)
Async XLA Ops:
  33.0 23.9 %copy-start = (f32[24,24]{1,0:T(8,128)S(1)}, f32[24,24]{1,0:T(8,128)}, u32[]{:S(2)}) copy-start(f32[24,24]{1,0:T(8,128)} %before.1) | copy-start | bytes 6916
  33.0 23.8 %copy-start.1 = (f32[24,24]{1,0:T(8,128)S(1)}, f32[24,24]{1,0:T(8,128)}, u32[]{:S(2)}) copy-start(f32[24,24]{1,0:T(8,128)} %after.1) | copy-start | bytes 6916
  56.8 0.7 copy-start.2
  56.8 0.7 copy-start.3

commit v3 on v2

--- a/solution.py
+++ b/solution.py
@@ -22,7 +22,7 @@
 SHORT = 16
 F32 = jnp.float32
 BF16 = jnp.bfloat16
-PARTS = 4
+PARTS = 1
 
 
 def iota(shape, dim):
@@ -83,7 +83,8 @@
     shard_start = jnp.sum(
         jnp.where(low & (own_col == own_row), len_col, 0.0), axis=0, keepdims=True
     )
-    info[...] = jnp.broadcast_to(shard_start, (8, TOK))
+    line = iota((8, TOK), 0)
+    info[...] = jnp.where(line == 0, shard_start, jnp.where(line == 1, len_row, own_row))
     packed = down(order[pl.ds(lax.axis_index("seq"), 1), :].astype(F32))
     inside = (packed >= start) & (packed < start + len_row)
 
@@ -173,28 +174,34 @@
     out[SHORT:] = jnp.where(fifth, jnp.broadcast_to(packed[:, None, :], long.shape), long)
 
 
-def mix(coefs, terms):
+def spread(coefs, table):
+    for j in range(HEADS):
+        table[j] = jnp.broadcast_to(coefs[:, j : j + 1], (HEADS, 128))
+
+
+def mix(table, terms):
     sums = []
     for j in range(HEADS):
-        total = coefs[0, j] * terms[0]
+        total = table[j, 0:1, :] * terms[0]
         for h in range(1, HEADS):
-            total = total + coefs[h, j] * terms[h]
+            total = total + table[j, h : h + 1, :] * terms[h]
         sums.append(total)
     return jnp.stack(sums)
 
 
-def soften_kernel(logits, before, after, lens, own, info, out):
+def soften_kernel(logits, before, after, info, out, table_b, table_a):
     owner = lax.axis_index("grp") * GROUP + lax.axis_index("sub")
-    shard = lax.axis_index("seq")
+    shard = lax.axis_index("seq").astype(F32)
+    spread(before, table_b)
+    spread(after, table_a)
     is_long = owner >= SHORT
     line = iota((8, 128), 0)
     lane = iota((8, 128), 1)
     slot = jnp.where(is_long, 128 + 4 * (owner - SHORT), 8 * owner) + line
     valid = jnp.logical_or(line < 4, jnp.logical_not(is_long))
-    begin = info[...]
-    length = lens[...].astype(F32)
+    begin, length, own = info[0:1, :], info[1:2, :], info[2:3, :]
     slot_f = slot.astype(F32)
-    held = (own[...] == shard) & (slot_f >= begin) & (slot_f < begin + length) & valid
+    held = (own == shard) & (slot_f >= begin) & (slot_f < begin + length) & valid
     filled = jnp.sum(jnp.where(held, 1.0, 0.0), axis=1, keepdims=True) > 0.5
     first = jnp.sum(jnp.where(held, begin, 0.0), axis=1, keepdims=True)
 
@@ -204,7 +211,7 @@
 
     main_ok = allowed(lane)
     tail_ok = allowed(128 + lane % 32) & is_long & (lane // 32 == line)
-    mixed = mix(before, [logits[h] for h in range(HEADS)])
+    mixed = mix(table_b, [logits[h] for h in range(HEADS)])
     tail = jnp.broadcast_to(mixed[:, 4:5, :], mixed.shape)
     main_m = jnp.where(main_ok[None], mixed, -1e30)
     tail_m = jnp.where(tail_ok[None], tail, -1e30)
@@ -212,12 +219,12 @@
     main_e = jnp.where(main_ok[None], jnp.exp(main_m - top), 0.0)
     tail_e = jnp.where(tail_ok[None], jnp.exp(tail_m - top), 0.0)
     total = jnp.sum(main_e + tail_e, axis=2, keepdims=True)
-    total = jnp.where(filled[None], total, 1.0)
-    main_w = (main_e / total).astype(BF16).astype(F32)
-    tail_w = (tail_e / total).astype(BF16).astype(F32)
+    share = 1.0 / jnp.where(filled[None], total, 1.0)
+    main_w = (main_e * share).astype(BF16).astype(F32)
+    tail_w = (tail_e * share).astype(BF16).astype(F32)
     tail_w = jnp.broadcast_to(jnp.sum(tail_w, axis=1, keepdims=True), tail_w.shape)
     weights = jnp.where(((line == 4) & is_long)[None], tail_w, main_w)
-    out[...] = mix(after, [weights[h] for h in range(HEADS)]).astype(BF16)
+    out[...] = mix(table_a, [weights[h] for h in range(HEADS)]).astype(BF16)
 
 
 def output_kernel(weights, values, out):
@@ -239,7 +246,6 @@
     grant = pltpu.CompilerParams(vmem_limit_bytes=12 << 20)
     rows = N_SEQ * PIECE
     vmem = pl.BlockSpec(memory_space=pltpu.VMEM)
-    smem = pl.BlockSpec(memory_space=pltpu.SMEM)
     pair = np.arange(HEAD_DIM) // 2
     freq = jnp.asarray((THETA ** (-2.0 * pair / HEAD_DIM)).astype(np.float32)[None, :])
     lens = doc_lengths.reshape(1, TOK)
@@ -297,12 +303,13 @@
     mine = lax.all_to_all(logits, ("grp", "sub"), split_axis=0, concat_axis=0, tiled=True)
     blended = pl.pallas_call(
         soften_kernel,
-        in_specs=[vmem, smem, smem, vmem, vmem, vmem],
+        in_specs=[vmem] * 4,
         out_specs=vmem,
         out_shape=jax.ShapeDtypeStruct((HEADS, 8, 128), BF16),
+        scratch_shapes=[pltpu.VMEM((HEADS, HEADS, 128), F32)] * 2,
         compiler_params=grant,
         name="soften",
-    )(mine, mix_before, mix_after, lens, own, info)
+    )(mine, mix_before, mix_after, info)
     back = lax.all_to_all(blended, ("grp", "sub"), split_axis=0, concat_axis=0, tiled=True)
     return pl.pallas_call(
         output_kernel,

time: 73.9 us -> 72.3 us (0.978)
  Pallas kernels: 5.72 us -> 4.81 us
    pallas_call x1, Pallas kernels: 1.66 us -> 0.73 us  [on_device(): pl.pallas_call(soften_kernel, in_specs=[vmem] * 4, out_specs=vmem, out_sh...]
where the time goes in v3:
time: 72.3 us; the launch traced here: 72 us
  blocking collectives  67.2 us (93%)
  Pallas kernels  4.81 us (7%)
    all_to_all x1, blocking collectives, on_device(): lax.all_to_all(logits, ('grp', 'sub'), split_axis=0, concat_axis=0, tiled...  23.8 us
    all_to_all x1, blocking collectives, on_device(): lax.all_to_all(send.reshape(N_SEQ, PIECE, 2 * HEAD_DIM), 'seq', split_axi...  19.6 us
    all_to_all x1, blocking collectives, on_device(): lax.all_to_all(blended, ('grp', 'sub'), split_axis=0, concat_axis=0, tile...  13.7 us
    all_gather x1, blocking collectives, on_device(): gathered = lax.all_gather(got[:, HEAD_DIM:], 'sub', axis=0, tiled=True)  10 us
    pallas_call x1, Pallas kernels, on_device(): pl.pallas_call(project_kernel, in_specs=[hbm] * 8, out_specs=[vmem, vmem]...  2.83 us

profile of v3, /device:TPU:1, one launch (start us, length us, event | category | flops | bytes accessed | tf_op | source)
XLA Modules:
  0.0 72.0 jit_solution(5463087789170945857)
XLA Ops:
  0.0 2.8 %project.1 = (bf16[256,256]{1,0:T(8,128)(2,1)S(1)}, f32[8,128]{1,0:T(8,128)S(1)}) custom-call(bf16[128,4096]{1,0:T(8,128)(2,1)} %hid_h.1, bf16[4096,128]{1,0:T(8,128)(2,1)} %wq_h.1, bf16[32,4096]{1,0:T(8,128)(2,1)} %bitcast.12, bf16[32,4096]{1,0:T(8,128)(2,1)} %bitcast.13, s32[1,128]{1,0:T(1,128)} %bitcast.15, s32[1,128]{1,0:T(1,128)} %bitcast.16, ...), custom_call_target="tpu_custom_call" | custom-call | tf_op jit(solution)/shard_map/project/pallas_call | solution.py:256
  2.8 19.6 %all_to_all.15 = bf16[32,8,256]{2,1,0:T(8,128)(2,1)S(1)} all-to-all(bf16[32,8,256]{2,1,0:T(8,128)(2,1)S(1)} %bitcast.11), channel_id=1, replica_groups=mesh['seq'=32,'grp'=6,'sub'=4] {'seq'}, dimensions={0} | all-to-all | bytes 262144 | tf_op jit(solution)/shard_map/all_to_all | solution.py:286
  22.5 10.0 %all_gather.3.gathered = bf16[1024,128]{1,0:T(8,128)(2,1)S(1)} all-gather(bf16[256,128]{1,0:T(8,128)(2,1)S(1)} %slice.4), channel_id=1, replica_groups=mesh['seq'=32,'grp'=6,'sub'=4] {'sub'}, dimensions={0}, use_global_device_ids=true | all-gather | bytes 327680 | tf_op jit(solution)/shard_map/all_gather | solution.py:289
  32.5 0.5 logits.1
  33.0 0.0 copy-start
  33.0 0.0 copy-start.1
  33.0 23.8 %all_to_all.16.logits = f32[24,8,128]{2,1,0:T(8,128)S(1)} all-to-all(f32[24,8,128]{2,1,0:T(8,128)S(1)} %get-tuple-element.10), channel_id=1, replica_groups=mesh['seq'=32,'grp'=6,'sub'=4] {'grp','sub'}, dimensions={0} | all-to-all | bytes 196608 | tf_op jit(solution)/shard_map/all_to_all | solution.py:303
  56.8 0.0 copy-done
  56.8 0.0 copy-done.1
  56.8 0.7 %soften.1 = bf16[24,8,128]{2,1,0:T(8,128)(2,1)S(1)} custom-call(f32[24,8,128]{2,1,0:T(8,128)S(1)} %all_to_all.16.logits, f32[24,24]{1,0:T(8,128)S(1)} %copy-done, f32[24,24]{1,0:T(8,128)S(1)} %copy-done.1, f32[8,128]{1,0:T(8,128)S(1)} %get-tuple-element.11.info), custom_call_target="tpu_custom_call" | custom-call | tf_op jit(solution)/shard_map/soften/pallas_call | solution.py:304
  57.6 13.7 %all_to_all.17 = bf16[24,8,128]{2,1,0:T(8,128)(2,1)S(1)} all-to-all(bf16[24,8,128]{2,1,0:T(8,128)(2,1)S(1)} %soften.1), channel_id=1, replica_groups=mesh['seq'=32,'grp'=6,'sub'=4] {'grp','sub'}, dimensions={0} | all-to-all | bytes 98304 | tf_op jit(solution)/shard_map/all_to_all | solution.py:313
  71.2 0.8 %output.1 = bf16[160,128]{1,0:T(8,128)(2,1)} custom-call(bf16[192,128]{1,0:T(8,128)(2,1)S(1)} %bitcast.10, bf16[256,128]{1,0:T(8,128)(2,1)S(1)} %get-tuple-element.12.values), custom_call_target="tpu_custom_call" | custom-call | tf_op jit(solution)/shard_map/output/pallas_call | solution.py:314
  (1 shorter events, 0.0 us)
Async XLA Ops:
  33.0 23.8 %copy-start = (f32[24,24]{1,0:T(8,128)S(1)}, f32[24,24]{1,0:T(8,128)}, u32[]{:S(2)}) copy-start(f32[24,24]{1,0:T(8,128)} %before.1) | copy-start | bytes 6916
  33.0 23.8 %copy-start.1 = (f32[24,24]{1,0:T(8,128)S(1)}, f32[24,24]{1,0:T(8,128)}, u32[]{:S(2)}) copy-start(f32[24,24]{1,0:T(8,128)} %after.1) | copy-start | bytes 6916

commit v4 on v3

--- a/solution.py
+++ b/solution.py
@@ -18,11 +18,11 @@
 TOK = 128
 CAP = 160
 PIECE = 8
-META = 5
+KV_ROW = 5
+META = 7
 SHORT = 16
 F32 = jnp.float32
 BF16 = jnp.bfloat16
-PARTS = 1
 
 
 def iota(shape, dim):
@@ -35,6 +35,10 @@
 
 def dot_nn(a, b):
     return lax.dot_general(a, b, (((1,), (0,)), ((), ())), preferred_element_type=F32)
+
+
+def turn(shape, sub):
+    return (iota(shape, len(shape) - 1) - KV_COLS * sub) & (HEAD_DIM - 1)
 
 
 def project_kernel(
@@ -42,7 +46,6 @@
     hid, wq, wkv, lens, own, order, freq, cos_t, sin_t, place, sems,
 ):
     sub = lax.axis_index("sub")
-    part = hid.shape[1] // PARTS
     copies = []
 
     def copy(source, target):
@@ -53,15 +56,11 @@
     copy(own_h, own)
     copy(order_h, order)
     copy(freq_h, freq)
-    for k in range(PARTS):
-        span = pl.ds(k * part, part)
-        copy(hid_h.at[:, span], hid.at[:, span])
-        copy(wq_h.at[span, :], wq.at[span, :])
-        copy(wk_h.at[:, span], wkv.at[pl.ds(0, KV_COLS), span])
-        copy(wv_h.at[:, span], wkv.at[pl.ds(2 * KV_COLS, KV_COLS), span])
-    blank = jnp.zeros((KV_COLS, hid.shape[1]), BF16)
-    wkv[KV_COLS : 2 * KV_COLS, :] = blank
-    wkv[3 * KV_COLS :, :] = blank
+    copy(hid_h, hid)
+    copy(wq_h, wq)
+    copy(wk_h, wkv.at[pl.ds(0, KV_COLS), :])
+    copy(wv_h, wkv.at[pl.ds(KV_COLS, KV_COLS), :])
+    wkv[2 * KV_COLS :, :] = jnp.zeros((2 * KV_COLS, hid.shape[1]), BF16)
     for k in range(4):
         copies[k].wait()
 
@@ -98,25 +97,29 @@
     rank = jnp.sum(
         jnp.where((target_row == target) & (col < row), 1.0, 0.0), axis=1, keepdims=True
     )
-    send_row = across(target * PIECE + rank)
+    pair = jnp.floor(rank * 0.5)
     angle = position * freq[...]
     cos_t[...] = jnp.cos(angle)
     sin_t[...] = jnp.sin(angle)
     rows = iota((N_SEQ * PIECE, TOK), 0).astype(F32)
-    place[:, :TOK] = jnp.where(rows == send_row, 1.0, 0.0).astype(BF16)
-    place[:, TOK:] = jnp.where(rows == target_row * PIECE + META, 1.0, 0.0).astype(BF16)
-    meta = jnp.where(col.astype(F32) == rank, slot + 1.0, 0.0).astype(BF16)
-
-    acc_q = jnp.zeros((TOK, HEAD_DIM), F32)
-    acc_kv = jnp.zeros((TOK, HEAD_DIM), F32)
-    for k in range(PARTS):
-        for c in copies[4 + 4 * k : 8 + 4 * k]:
-            c.wait()
-        block = hid[:, k * part : (k + 1) * part]
-        acc_q = acc_q + dot_nn(block, wq[k * part : (k + 1) * part, :])
-        acc_kv = acc_kv + dot_nt(block, wkv[:, k * part : (k + 1) * part])
-
+
+    def put(k, where_to):
+        place[:, k * TOK : (k + 1) * TOK] = jnp.where(rows == where_to, 1.0, 0.0).astype(BF16)
+
+    put(0, across(target * PIECE + rank))
+    put(1, across(target * PIECE + KV_ROW + pair))
+    put(2, target_row * PIECE + META)
+    turned = turn(shape, sub)
+    meta = turned.astype(F32) == rank + HEAD_DIM // 2
+    meta = jnp.where(meta, slot + 1.0, 0.0).astype(BF16)
+    side = (turned // (HEAD_DIM // 2)).astype(F32) == rank - 2.0 * pair
+
+    for c in copies[4:]:
+        c.wait()
+    acc_q = dot_nn(hid[...], wq[...])
+    acc_kv = dot_nt(hid[...], wkv[...])
     even = col % 2 == 0
+
     cos_a, sin_a = cos_t[...], sin_t[...]
 
     def rope(value):
@@ -125,42 +128,52 @@
 
     query = rope(acc_q).astype(BF16)
     kv = pltpu.roll(acc_kv, KV_COLS * sub, 1)
-    kv = jnp.where(col // KV_COLS == sub, rope(kv), kv).astype(BF16)
-    spots = place[...]
-    send[:, :HEAD_DIM] = dot_nn(spots, jnp.concatenate([query, meta], axis=0)).astype(BF16)
-    send[:, HEAD_DIM:] = dot_nn(spots[:, :TOK], kv).astype(BF16)
+    kv = jnp.where(turned < KV_COLS, rope(kv), kv)
+    kv = jnp.where(side, kv + pltpu.roll(kv, HEAD_DIM // 2, 1), 0.0).astype(BF16)
+    send[...] = dot_nn(place[...], jnp.concatenate([query, kv, meta], axis=0)).astype(BF16)
 
 
 def logits_kernel(scale, got, gathered, out, values):
     rows = N_SEQ * PIECE
-    mine = got[:, :HEAD_DIM]
+    mine = got[...]
     head = mine.astype(F32).reshape(N_SEQ, PIECE, HEAD_DIM)
     tags = jnp.broadcast_to(head[:, META : META + 1, :], head.shape)
-    hit = iota(head.shape, 2) == iota(head.shape, 1)
-    slot_col = jnp.sum(jnp.where(hit, tags, 0.0), axis=2, keepdims=True).reshape(rows, 1) - 1.0
+    line, lane = iota(head.shape, 1), turn(head.shape, lax.axis_index("sub")) - HEAD_DIM // 2
     same = iota((rows, rows), 0) == iota((rows, rows), 1)
-    slot_row = jnp.sum(jnp.where(same, slot_col, 0.0), axis=0, keepdims=True)
+
+    token = jnp.where(line < KV_ROW, line, 2 * (line - KV_ROW))
+    weight = jnp.where((lane == token + 1) & (line >= KV_ROW) & (line < META), 256.0, 0.0)
+    weight = jnp.where(lane == token, 1.0, weight)
+    column = jnp.sum(weight * tags, axis=2, keepdims=True).reshape(rows, 1)
+    both = jnp.sum(jnp.where(same, column, 0.0), axis=0, keepdims=True)
+    right = jnp.floor(both * (1.0 / 256.0))
+    left, right = both - 256.0 * right - 1.0, right - 1.0
+    is_query = iota((1, rows), 1) % PIECE < KV_ROW
 
     window = iota((rows, HEAD_DIM), 1) // KV_COLS
-    key = jnp.zeros((rows, HEAD_DIM), F32)
-    value = jnp.zeros((rows, HEAD_DIM), F32)
+    blocks = [jnp.zeros((rows, HEAD_DIM), F32)] * 4
     for c in range(GROUP):
         tile = gathered[c * rows : (c + 1) * rows, :].astype(F32)
-        key = jnp.where(window == c, tile, key)
-        value = jnp.where(window == (c + 2) % GROUP, tile, value)
-    value = pltpu.roll(value, HEAD_DIM // 2, 1)
+        for i in range(4):
+            blocks[i] = jnp.where(window == (c + i) % GROUP, tile, blocks[i])
+    for i in range(1, 4):
+        blocks[i] = pltpu.roll(blocks[i], HEAD_DIM - i * KV_COLS, 1)
+    key = jnp.concatenate([blocks[0].astype(BF16), blocks[2].astype(BF16)], axis=0)
+    value = jnp.concatenate([blocks[1].astype(BF16), blocks[3].astype(BF16)], axis=0)
 
     n = iota((rows, 1), 0)
     kv_slot = jnp.where(n < 128, n, 128 + n % 32).astype(F32)
-    kv_spots = jnp.where(kv_slot == slot_row, 1.0, 0.0).astype(BF16)
+    from_left = jnp.where(kv_slot == jnp.where(is_query, -1.0, left), 1.0, 0.0).astype(BF16)
+    from_right = jnp.where(kv_slot == right, 1.0, 0.0).astype(BF16)
+    kv_spots = jnp.concatenate([from_left, from_right], axis=1)
     n = iota((224, 1), 0)
     late = jnp.where(n % 8 < 4, 64 + n // 8 * 4 + n % 8, -5)
     strided = 128 + 4 * (n % 8) + (n - 192) // 8
     q_slot = jnp.where(n < 128, n, jnp.where(n < 192, late, strided)).astype(F32)
-    q_spots = jnp.where(q_slot == slot_row, 1.0, 0.0).astype(BF16)
+    q_spots = jnp.where(q_slot == jnp.where(is_query, left, -1.0), 1.0, 0.0).astype(BF16)
     query = dot_nn(q_spots, mine).astype(BF16)
-    key = dot_nn(kv_spots, key.astype(BF16)).astype(BF16)
-    values[...] = dot_nn(kv_spots, value.astype(BF16)).astype(BF16)
+    key = dot_nn(kv_spots, key).astype(BF16)
+    values[...] = dot_nn(kv_spots, value).astype(BF16)
 
     main = dot_nt(query[:192], key[:128]) * scale
     tail = dot_nt(query[192:], key[128:]) * scale
@@ -258,7 +271,7 @@
         in_specs=[hbm] * 8,
         out_specs=[vmem, vmem],
         out_shape=[
-            jax.ShapeDtypeStruct((rows, 2 * HEAD_DIM), BF16),
+            jax.ShapeDtypeStruct((rows, HEAD_DIM), BF16),
             jax.ShapeDtypeStruct((8, TOK), F32),
         ],
         scratch_shapes=[
@@ -271,8 +284,8 @@
             pltpu.VMEM((1, TOK), F32),
             pltpu.VMEM((TOK, HEAD_DIM), F32),
             pltpu.VMEM((TOK, HEAD_DIM), F32),
-            pltpu.VMEM((rows, 2 * TOK), BF16),
-            pltpu.SemaphoreType.DMA((4 + 4 * PARTS,)),
+            pltpu.VMEM((rows, 3 * TOK), BF16),
+            pltpu.SemaphoreType.DMA((8,)),
         ],
         compiler_params=grant,
         name="project",
@@ -284,9 +297,9 @@
     )
 
     got = lax.all_to_all(
-        send.reshape(N_SEQ, PIECE, 2 * HEAD_DIM), "seq", split_axis=0, concat_axis=0, tiled=True
-    ).reshape(rows, 2 * HEAD_DIM)
-    gathered = lax.all_gather(got[:, HEAD_DIM:], "sub", axis=0, tiled=True)
+        send.reshape(N_SEQ, PIECE, HEAD_DIM), "seq", split_axis=0, concat_axis=0, tiled=True
+    ).reshape(rows, HEAD_DIM)
+    gathered = lax.all_gather(got, "sub", axis=0, tiled=True)
 
     logits, values = pl.pallas_call(
         functools.partial(logits_kernel, 1.0 / HEAD_DIM**0.5),

time: 72.3 us -> 72 us (level)
  no operation moved by 1% of the time
where the time goes in v4:
time: 72 us; the launch traced here: 71.8 us
  blocking collectives  66.7 us (93%)
  Pallas kernels  5.04 us (7%)
    all_to_all x1, blocking collectives, on_device(): lax.all_to_all(logits, ('grp', 'sub'), split_axis=0, concat_axis=0, tiled...  23.9 us
    all_to_all x1, blocking collectives, on_device(): lax.all_to_all(send.reshape(N_SEQ, PIECE, HEAD_DIM), 'seq', split_axis=0,...  19.1 us
    all_to_all x1, blocking collectives, on_device(): lax.all_to_all(blended, ('grp', 'sub'), split_axis=0, concat_axis=0, tile...  13.7 us
    all_gather x1, blocking collectives, on_device(): gathered = lax.all_gather(got, 'sub', axis=0, tiled=True)  9.95 us
    pallas_call x1, Pallas kernels, on_device(): pl.pallas_call(project_kernel, in_specs=[hbm] * 8, out_specs=[vmem, vmem]...  2.97 us

profile of v4, /device:TPU:1, one launch (start us, length us, event | category | flops | bytes accessed | tf_op | source)
XLA Modules:
  0.0 71.8 jit_solution(15526573000980245)
XLA Ops:
  0.0 3.0 %project.1 = (bf16[256,128]{1,0:T(8,128)(2,1)S(1)}, f32[8,128]{1,0:T(8,128)S(1)}) custom-call(bf16[128,4096]{1,0:T(8,128)(2,1)} %hid_h.1, bf16[4096,128]{1,0:T(8,128)(2,1)} %wq_h.1, bf16[32,4096]{1,0:T(8,128)(2,1)} %bitcast.12, bf16[32,4096]{1,0:T(8,128)(2,1)} %bitcast.13, s32[1,128]{1,0:T(1,128)} %bitcast.15, s32[1,128]{1,0:T(1,128)} %bitcast.16, ...), custom_call_target="tpu_custom_call" | custom-call | tf_op jit(solution)/shard_map/project/pallas_call | solution.py:269
  3.0 19.1 %all_to_all.15 = bf16[32,8,128]{2,1,0:T(8,128)(2,1)S(1)} all-to-all(bf16[32,8,128]{2,1,0:T(8,128)(2,1)S(1)} %bitcast.11), channel_id=1, replica_groups=mesh['seq'=32,'grp'=6,'sub'=4] {'seq'}, dimensions={0} | all-to-all | bytes 131072 | tf_op jit(solution)/shard_map/all_to_all | solution.py:299
  22.1 10.0 %all_gather.3.gathered = bf16[1024,128]{1,0:T(8,128)(2,1)S(1)} all-gather(bf16[256,128]{1,0:T(8,128)(2,1)S(1)} %bitcast.8), channel_id=1, replica_groups=mesh['seq'=32,'grp'=6,'sub'=4] {'sub'}, dimensions={0}, use_global_device_ids=true | all-gather | bytes 327680 | tf_op jit(solution)/shard_map/all_gather | solution.py:302
  32.0 0.6 logits.1
  32.6 0.0 copy-start
  32.6 0.0 copy-start.1
  32.6 23.9 %all_to_all.16.logits = f32[24,8,128]{2,1,0:T(8,128)S(1)} all-to-all(f32[24,8,128]{2,1,0:T(8,128)S(1)} %get-tuple-element.10), channel_id=1, replica_groups=mesh['seq'=32,'grp'=6,'sub'=4] {'grp','sub'}, dimensions={0} | all-to-all | bytes 196608 | tf_op jit(solution)/shard_map/all_to_all | solution.py:316
  56.6 0.0 copy-done
  56.6 0.0 copy-done.1
  56.6 0.7 %soften.1 = bf16[24,8,128]{2,1,0:T(8,128)(2,1)S(1)} custom-call(f32[24,8,128]{2,1,0:T(8,128)S(1)} %all_to_all.16.logits, f32[24,24]{1,0:T(8,128)S(1)} %copy-done, f32[24,24]{1,0:T(8,128)S(1)} %copy-done.1, f32[8,128]{1,0:T(8,128)S(1)} %get-tuple-element.11.info), custom_call_target="tpu_custom_call" | custom-call | tf_op jit(solution)/shard_map/soften/pallas_call | solution.py:317
  57.3 13.7 %all_to_all.17 = bf16[24,8,128]{2,1,0:T(8,128)(2,1)S(1)} all-to-all(bf16[24,8,128]{2,1,0:T(8,128)(2,1)S(1)} %soften.1), channel_id=1, replica_groups=mesh['seq'=32,'grp'=6,'sub'=4] {'grp','sub'}, dimensions={0} | all-to-all | bytes 98304 | tf_op jit(solution)/shard_map/all_to_all | solution.py:326
  71.0 0.8 %output.1 = bf16[160,128]{1,0:T(8,128)(2,1)} custom-call(bf16[192,128]{1,0:T(8,128)(2,1)S(1)} %bitcast.10, bf16[256,128]{1,0:T(8,128)(2,1)S(1)} %get-tuple-element.12.values), custom_call_target="tpu_custom_call" | custom-call | tf_op jit(solution)/shard_map/output/pallas_call | solution.py:327
Async XLA Ops:
  32.6 24.0 %copy-start = (f32[24,24]{1,0:T(8,128)S(1)}, f32[24,24]{1,0:T(8,128)}, u32[]{:S(2)}) copy-start(f32[24,24]{1,0:T(8,128)} %before.1) | copy-start | bytes 6916
  32.6 23.9 %copy-start.1 = (f32[24,24]{1,0:T(8,128)S(1)}, f32[24,24]{1,0:T(8,128)}, u32[]{:S(2)}) copy-start(f32[24,24]{1,0:T(8,128)} %after.1) | copy-start | bytes 6916

commit v5 on v4

--- a/solution.py
+++ b/solution.py
@@ -43,7 +43,7 @@
 
 def project_kernel(
     hid_h, wq_h, wk_h, wv_h, lens_h, own_h, order_h, freq_h, send, info,
-    hid, wq, wkv, lens, own, order, freq, cos_t, sin_t, place, sems,
+    hid, wq, wkv, lens, own, order, freq, cos_t, sin_t, first, place, sems,
 ):
     sub = lax.axis_index("sub")
     copies = []
@@ -56,10 +56,13 @@
     copy(own_h, own)
     copy(order_h, order)
     copy(freq_h, freq)
-    copy(hid_h, hid)
-    copy(wq_h, wq)
-    copy(wk_h, wkv.at[pl.ds(0, KV_COLS), :])
-    copy(wv_h, wkv.at[pl.ds(KV_COLS, KV_COLS), :])
+    half = hid.shape[1] // 2
+    for part in range(2):
+        span = pl.ds(part * half, half)
+        copy(hid_h.at[:, span], hid.at[:, span])
+        copy(wq_h.at[span, :], wq.at[span, :])
+        copy(wk_h.at[:, span], wkv.at[pl.ds(0, KV_COLS), span])
+        copy(wv_h.at[:, span], wkv.at[pl.ds(KV_COLS, KV_COLS), span])
     wkv[2 * KV_COLS :, :] = jnp.zeros((2 * KV_COLS, hid.shape[1]), BF16)
     for k in range(4):
         copies[k].wait()
@@ -100,7 +103,9 @@
     pair = jnp.floor(rank * 0.5)
     angle = position * freq[...]
     cos_t[...] = jnp.cos(angle)
-    sin_t[...] = jnp.sin(angle)
+    even = col % 2 == 0
+    sin = jnp.sin(angle)
+    sin_t[...] = jnp.where(even, -sin, sin)
     rows = iota((N_SEQ * PIECE, TOK), 0).astype(F32)
 
     def put(k, where_to):
@@ -114,16 +119,20 @@
     meta = jnp.where(meta, slot + 1.0, 0.0).astype(BF16)
     side = (turned // (HEAD_DIM // 2)).astype(F32) == rank - 2.0 * pair
 
-    for c in copies[4:]:
+    for c in copies[4:8]:
         c.wait()
-    acc_q = dot_nn(hid[...], wq[...])
-    acc_kv = dot_nt(hid[...], wkv[...])
+    first[0] = dot_nn(hid[:, :half], wq[:half, :])
+    first[1] = dot_nt(hid[:, :half], wkv[:, :half])
+    for c in copies[8:]:
+        c.wait()
+    acc_q = first[0] + dot_nn(hid[:, half:], wq[half:, :])
+    acc_kv = first[1] + dot_nt(hid[:, half:], wkv[:, half:])
     even = col % 2 == 0
 
     cos_a, sin_a = cos_t[...], sin_t[...]
 
     def rope(value):
-        partner = jnp.where(even, -pltpu.roll(value, HEAD_DIM - 1, 1), pltpu.roll(value, 1, 1))
+        partner = jnp.where(even, pltpu.roll(value, HEAD_DIM - 1, 1), pltpu.roll(value, 1, 1))
         return value * cos_a + partner * sin_a
 
     query = rope(acc_q).astype(BF16)
@@ -284,8 +293,9 @@
             pltpu.VMEM((1, TOK), F32),
             pltpu.VMEM((TOK, HEAD_DIM), F32),
             pltpu.VMEM((TOK, HEAD_DIM), F32),
+            pltpu.VMEM((2, TOK, HEAD_DIM), F32),
             pltpu.VMEM((rows, 3 * TOK), BF16),
-            pltpu.SemaphoreType.DMA((8,)),
+            pltpu.SemaphoreType.DMA((12,)),
         ],
         compiler_params=grant,
         name="project",

time: 72 us -> 71.7 us (level)
  no operation moved by 1% of the time
where the time goes in v5:
time: 71.7 us; the launch traced here: 71.5 us
  blocking collectives  66.7 us (93%)
  Pallas kernels  4.74 us (7%)
    all_to_all x1, blocking collectives, on_device(): lax.all_to_all(logits, ('grp', 'sub'), split_axis=0, concat_axis=0, tiled...  23.9 us
    all_to_all x1, blocking collectives, on_device(): lax.all_to_all(send.reshape(N_SEQ, PIECE, HEAD_DIM), 'seq', split_axis=0,...  19.1 us
    all_to_all x1, blocking collectives, on_device(): lax.all_to_all(blended, ('grp', 'sub'), split_axis=0, concat_axis=0, tile...  13.7 us
    all_gather x1, blocking collectives, on_device(): gathered = lax.all_gather(got, 'sub', axis=0, tiled=True)  9.95 us
    pallas_call x1, Pallas kernels, on_device(): pl.pallas_call(project_kernel, in_specs=[hbm] * 8, out_specs=[vmem, vmem]...  2.68 us

profile of v5, /device:TPU:1, one launch (start us, length us, event | category | flops | bytes accessed | tf_op | source)
XLA Modules:
  0.0 71.5 jit_solution(1370757585161374287)
XLA Ops:
  0.0 2.7 %project.1 = (bf16[256,128]{1,0:T(8,128)(2,1)S(1)}, f32[8,128]{1,0:T(8,128)S(1)}) custom-call(bf16[128,4096]{1,0:T(8,128)(2,1)} %hid_h.1, bf16[4096,128]{1,0:T(8,128)(2,1)} %wq_h.1, bf16[32,4096]{1,0:T(8,128)(2,1)} %bitcast.12, bf16[32,4096]{1,0:T(8,128)(2,1)} %bitcast.13, s32[1,128]{1,0:T(1,128)} %bitcast.15, s32[1,128]{1,0:T(1,128)} %bitcast.16, ...), custom_call_target="tpu_custom_call" | custom-call | tf_op jit(solution)/shard_map/project/pallas_call | solution.py:278
  2.7 19.1 %all_to_all.15 = bf16[32,8,128]{2,1,0:T(8,128)(2,1)S(1)} all-to-all(bf16[32,8,128]{2,1,0:T(8,128)(2,1)S(1)} %bitcast.11), channel_id=1, replica_groups=mesh['seq'=32,'grp'=6,'sub'=4] {'seq'}, dimensions={0} | all-to-all | bytes 131072 | tf_op jit(solution)/shard_map/all_to_all | solution.py:309
  21.8 10.0 %all_gather.3.gathered = bf16[1024,128]{1,0:T(8,128)(2,1)S(1)} all-gather(bf16[256,128]{1,0:T(8,128)(2,1)S(1)} %bitcast.8), channel_id=1, replica_groups=mesh['seq'=32,'grp'=6,'sub'=4] {'sub'}, dimensions={0}, use_global_device_ids=true | all-gather | bytes 327680 | tf_op jit(solution)/shard_map/all_gather | solution.py:312
  31.8 0.6 logits.1
  32.3 0.0 copy-start
  32.3 0.0 copy-start.1
  32.3 23.9 %all_to_all.16.logits = f32[24,8,128]{2,1,0:T(8,128)S(1)} all-to-all(f32[24,8,128]{2,1,0:T(8,128)S(1)} %get-tuple-element.10), channel_id=1, replica_groups=mesh['seq'=32,'grp'=6,'sub'=4] {'grp','sub'}, dimensions={0} | all-to-all | bytes 196608 | tf_op jit(solution)/shard_map/all_to_all | solution.py:326
  56.3 0.0 copy-done
  56.3 0.0 copy-done.1
  56.3 0.7 %soften.1 = bf16[24,8,128]{2,1,0:T(8,128)(2,1)S(1)} custom-call(f32[24,8,128]{2,1,0:T(8,128)S(1)} %all_to_all.16.logits, f32[24,24]{1,0:T(8,128)S(1)} %copy-done, f32[24,24]{1,0:T(8,128)S(1)} %copy-done.1, f32[8,128]{1,0:T(8,128)S(1)} %get-tuple-element.11.info), custom_call_target="tpu_custom_call" | custom-call | tf_op jit(solution)/shard_map/soften/pallas_call | solution.py:327
  57.0 13.7 %all_to_all.17 = bf16[24,8,128]{2,1,0:T(8,128)(2,1)S(1)} all-to-all(bf16[24,8,128]{2,1,0:T(8,128)(2,1)S(1)} %soften.1), channel_id=1, replica_groups=mesh['seq'=32,'grp'=6,'sub'=4] {'grp','sub'}, dimensions={0} | all-to-all | bytes 98304 | tf_op jit(solution)/shard_map/all_to_all | solution.py:336
  70.7 0.8 %output.1 = bf16[160,128]{1,0:T(8,128)(2,1)} custom-call(bf16[192,128]{1,0:T(8,128)(2,1)S(1)} %bitcast.10, bf16[256,128]{1,0:T(8,128)(2,1)S(1)} %get-tuple-element.12.values), custom_call_target="tpu_custom_call" | custom-call | tf_op jit(solution)/shard_map/output/pallas_call | solution.py:337
Async XLA Ops:
  32.3 24.0 %copy-start = (f32[24,24]{1,0:T(8,128)S(1)}, f32[24,24]{1,0:T(8,128)}, u32[]{:S(2)}) copy-start(f32[24,24]{1,0:T(8,128)} %before.1) | copy-start | bytes 6916
  32.3 23.9 %copy-start.1 = (f32[24,24]{1,0:T(8,128)S(1)}, f32[24,24]{1,0:T(8,128)}, u32[]{:S(2)}) copy-start(f32[24,24]{1,0:T(8,128)} %after.1) | copy-start | bytes 6916

commit v6 on v5

--- a/solution.py
+++ b/solution.py
@@ -19,6 +19,7 @@
 CAP = 160
 PIECE = 8
 KV_ROW = 5
+KV_ROWS = 4
 META = 7
 SHORT = 16
 F32 = jnp.float32
@@ -148,21 +149,28 @@
     head = mine.astype(F32).reshape(N_SEQ, PIECE, HEAD_DIM)
     tags = jnp.broadcast_to(head[:, META : META + 1, :], head.shape)
     line, lane = iota(head.shape, 1), turn(head.shape, lax.axis_index("sub")) - HEAD_DIM // 2
-    same = iota((rows, rows), 0) == iota((rows, rows), 1)
-
     token = jnp.where(line < KV_ROW, line, 2 * (line - KV_ROW))
     weight = jnp.where((lane == token + 1) & (line >= KV_ROW) & (line < META), 256.0, 0.0)
     weight = jnp.where(lane == token, 1.0, weight)
     column = jnp.sum(weight * tags, axis=2, keepdims=True).reshape(rows, 1)
-    both = jnp.sum(jnp.where(same, column, 0.0), axis=0, keepdims=True)
+
+    def across(shape, target):
+        hit = iota(shape, 0) == target
+        return jnp.sum(jnp.where(hit, column, 0.0), axis=0, keepdims=True)
+
+    n = iota((rows, rows), 1)
+    query_slot = across((rows, rows), jnp.where(n % PIECE < KV_ROW, n, -1)) - 1.0
+    kv_rows = N_SEQ * KV_ROWS
+    n = iota((rows, kv_rows), 1)
+    n = jnp.where(n % KV_ROWS > 0, n // KV_ROWS * PIECE + PIECE - KV_ROWS + n % KV_ROWS, -1)
+    both = across((rows, kv_rows), n)
     right = jnp.floor(both * (1.0 / 256.0))
     left, right = both - 256.0 * right - 1.0, right - 1.0
-    is_query = iota((1, rows), 1) % PIECE < KV_ROW
-
-    window = iota((rows, HEAD_DIM), 1) // KV_COLS
-    blocks = [jnp.zeros((rows, HEAD_DIM), F32)] * 4
+
+    window = iota((kv_rows, HEAD_DIM), 1) // KV_COLS
+    blocks = [jnp.zeros((kv_rows, HEAD_DIM), F32)] * 4
     for c in range(GROUP):
-        tile = gathered[c * rows : (c + 1) * rows, :].astype(F32)
+        tile = gathered[c * kv_rows : (c + 1) * kv_rows, :].astype(F32)
         for i in range(4):
             blocks[i] = jnp.where(window == (c + i) % GROUP, tile, blocks[i])
     for i in range(1, 4):
@@ -172,14 +180,14 @@
 
     n = iota((rows, 1), 0)
     kv_slot = jnp.where(n < 128, n, 128 + n % 32).astype(F32)
-    from_left = jnp.where(kv_slot == jnp.where(is_query, -1.0, left), 1.0, 0.0).astype(BF16)
+    from_left = jnp.where(kv_slot == left, 1.0, 0.0).astype(BF16)
     from_right = jnp.where(kv_slot == right, 1.0, 0.0).astype(BF16)
     kv_spots = jnp.concatenate([from_left, from_right], axis=1)
     n = iota((224, 1), 0)
     late = jnp.where(n % 8 < 4, 64 + n // 8 * 4 + n % 8, -5)
     strided = 128 + 4 * (n % 8) + (n - 192) // 8
     q_slot = jnp.where(n < 128, n, jnp.where(n < 192, late, strided)).astype(F32)
-    q_spots = jnp.where(q_slot == jnp.where(is_query, left, -1.0), 1.0, 0.0).astype(BF16)
+    q_spots = jnp.where(q_slot == query_slot, 1.0, 0.0).astype(BF16)
     query = dot_nn(q_spots, mine).astype(BF16)
     key = dot_nn(kv_spots, key).astype(BF16)
     values[...] = dot_nn(kv_spots, value).astype(BF16)
@@ -308,8 +316,10 @@
 
     got = lax.all_to_all(
         send.reshape(N_SEQ, PIECE, HEAD_DIM), "seq", split_axis=0, concat_axis=0, tiled=True
-    ).reshape(rows, HEAD_DIM)
-    gathered = lax.all_gather(got, "sub", axis=0, tiled=True)
+    )
+    gathered = lax.all_gather(got[:, PIECE - KV_ROWS :], "sub", axis=0, tiled=True)
+    got = got.reshape(rows, HEAD_DIM)
+    gathered = gathered.reshape(GROUP * N_SEQ * KV_ROWS, HEAD_DIM)
 
     logits, values = pl.pallas_call(
         functools.partial(logits_kernel, 1.0 / HEAD_DIM**0.5),

time: 71.7 us -> 71.4 us (level)
  no operation moved by 1% of the time
where the time goes in v6:
time: 71.4 us; the launch traced here: 71.1 us
  blocking collectives  66.3 us (93%)
  Pallas kernels  4.68 us (7%)
    all_to_all x1, blocking collectives, on_device(): lax.all_to_all(logits, ('grp', 'sub'), split_axis=0, concat_axis=0, tiled...  23.9 us
    all_to_all x1, blocking collectives, on_device(): lax.all_to_all(send.reshape(N_SEQ, PIECE, HEAD_DIM), 'seq', split_axis=0,...  19.1 us
    all_to_all x1, blocking collectives, on_device(): lax.all_to_all(blended, ('grp', 'sub'), split_axis=0, concat_axis=0, tile...  13.7 us
    all_gather x1, blocking collectives, on_device(): lax.all_gather(got[:, PIECE - KV_ROWS:], 'sub', axis=0, tiled=True)  9.61 us
    pallas_call x1, Pallas kernels, on_device(): pl.pallas_call(project_kernel, in_specs=[hbm] * 8, out_specs=[vmem, vmem]...  2.68 us

profile of v6, /device:TPU:1, one launch (start us, length us, event | category | flops | bytes accessed | tf_op | source)
XLA Modules:
  0.0 71.1 jit_solution(5160412106189811259)
XLA Ops:
  0.0 2.7 %project.1 = (bf16[256,128]{1,0:T(8,128)(2,1)S(1)}, f32[8,128]{1,0:T(8,128)S(1)}) custom-call(bf16[128,4096]{1,0:T(8,128)(2,1)} %hid_h.1, bf16[4096,128]{1,0:T(8,128)(2,1)} %wq_h.1, bf16[32,4096]{1,0:T(8,128)(2,1)} %bitcast.13, bf16[32,4096]{1,0:T(8,128)(2,1)} %bitcast.14, s32[1,128]{1,0:T(1,128)} %bitcast.16, s32[1,128]{1,0:T(1,128)} %bitcast.17, ...), custom_call_target="tpu_custom_call" | custom-call | tf_op jit(solution)/shard_map/project/pallas_call | solution.py:286
  2.7 19.1 %all_to_all.15 = bf16[32,8,128]{2,1,0:T(8,128)(2,1)S(1)} all-to-all(bf16[32,8,128]{2,1,0:T(8,128)(2,1)S(1)} %bitcast.12), channel_id=1, replica_groups=mesh['seq'=32,'grp'=6,'sub'=4] {'seq'}, dimensions={0} | all-to-all | bytes 131072 | tf_op jit(solution)/shard_map/all_to_all | solution.py:317
  21.8 9.6 %all_gather.3 = bf16[128,4,128]{2,1,0:T(4,128)(2,1)S(1)} all-gather(bf16[32,4,128]{2,1,0:T(4,128)(2,1)S(1)} %slice.4), channel_id=1, replica_groups=mesh['seq'=32,'grp'=6,'sub'=4] {'sub'}, dimensions={0}, use_global_device_ids=true | all-gather | bytes 163840 | tf_op jit(solution)/shard_map/all_gather | solution.py:320
  31.4 0.5 logits.1
  31.9 0.0 copy-start
  31.9 0.0 copy-start.1
  31.9 23.9 %all_to_all.16.logits = f32[24,8,128]{2,1,0:T(8,128)S(1)} all-to-all(f32[24,8,128]{2,1,0:T(8,128)S(1)} %get-tuple-element.10), channel_id=1, replica_groups=mesh['seq'=32,'grp'=6,'sub'=4] {'grp','sub'}, dimensions={0} | all-to-all | bytes 196608 | tf_op jit(solution)/shard_map/all_to_all | solution.py:336
  55.9 0.0 copy-done
  55.9 0.0 copy-done.1
  55.9 0.7 %soften.1 = bf16[24,8,128]{2,1,0:T(8,128)(2,1)S(1)} custom-call(f32[24,8,128]{2,1,0:T(8,128)S(1)} %all_to_all.16.logits, f32[24,24]{1,0:T(8,128)S(1)} %copy-done, f32[24,24]{1,0:T(8,128)S(1)} %copy-done.1, f32[8,128]{1,0:T(8,128)S(1)} %get-tuple-element.11.info), custom_call_target="tpu_custom_call" | custom-call | tf_op jit(solution)/shard_map/soften/pallas_call | solution.py:337
  56.6 13.7 %all_to_all.17 = bf16[24,8,128]{2,1,0:T(8,128)(2,1)S(1)} all-to-all(bf16[24,8,128]{2,1,0:T(8,128)(2,1)S(1)} %soften.1), channel_id=1, replica_groups=mesh['seq'=32,'grp'=6,'sub'=4] {'grp','sub'}, dimensions={0} | all-to-all | bytes 98304 | tf_op jit(solution)/shard_map/all_to_all | solution.py:346
  70.3 0.8 %output.1 = bf16[160,128]{1,0:T(8,128)(2,1)} custom-call(bf16[192,128]{1,0:T(8,128)(2,1)S(1)} %bitcast.11, bf16[256,128]{1,0:T(8,128)(2,1)S(1)} %get-tuple-element.12.values), custom_call_target="tpu_custom_call" | custom-call | tf_op jit(solution)/shard_map/output/pallas_call | solution.py:347
  (1 shorter events, 0.0 us)
Async XLA Ops:
  31.9 24.0 %copy-start = (f32[24,24]{1,0:T(8,128)S(1)}, f32[24,24]{1,0:T(8,128)}, u32[]{:S(2)}) copy-start(f32[24,24]{1,0:T(8,128)} %before.1) | copy-start | bytes 6916
  31.9 23.9 %copy-start.1 = (f32[24,24]{1,0:T(8,128)S(1)}, f32[24,24]{1,0:T(8,128)}, u32[]{:S(2)}) copy-start(f32[24,24]{1,0:T(8,128)} %after.1) | copy-start | bytes 6916
